TPU v7x, 32 devices: a whole 2x2x4 slice. The times are simulated.
32 devices in a mesh: groups: 2 (over x), tensor: 16 (over z, y, core).
Axes of the slice: x: 2, y: 2, z: 4, core: 2. Of those that a mesh axis runs over, the one named last changes fastest.
Arguments:
- hidden_in: bfloat16 [256, 8192], P(('groups', 'tensor')), parts along dimension 0, may hold values from -6 to 6
- norm_gain: bfloat16 [8192], replicated, may hold values from 0.25 to 1.75
- w_query: bfloat16 [8192, 64, 128], P(None, 'tensor'), may hold values from -0.0625 to 0.0625
- w_kv: bfloat16 [8192, 8, 2, 128], P('tensor'), may hold values from -0.5 to 0.5
- w_out: bfloat16 [64, 128, 8192], P('tensor'), may hold values from -0.0625 to 0.0625
- prefix_keys: bfloat16 [32, 6, 2048, 128], P(('groups', 'tensor')), parts along dimension 0, may hold values from -1000 to 1000
- prefix_values: bfloat16 [32, 6, 2048, 128], P(('groups', 'tensor')), parts along dimension 0, may hold values from -6 to 6
- suffix_keys: bfloat16 [32, 126, 256, 128], P(('groups', 'tensor')), parts along dimension 0, may hold values from -10 to 10
- suffix_values: bfloat16 [32, 126, 256, 128], P(('groups', 'tensor')), parts along dimension 0, may hold values from -6 to 6
- row_counts: int32 [24], P('groups'), parts along dimension 0, may hold values from 1 to 21, 128 in all
- suffix_lengths: int32 [256], P('groups'), parts along dimension 0, may hold values from 1 to 256
Outputs:
- layer_out: bfloat16 [256, 8192], P(('groups', 'tensor')), parts along dimension 0
There are 2 independent parts, one for each index of `groups`. A program takes and returns all parts, laid end to end along the dimension named above; an argument that names none is the same for every part. Nothing has to cross between parts.
Inputs may be any that keep to these rules, and one draw needn't show every extreme that they name: `row_counts`: critique rows are stored prompt by prompt: the rows of prompt p follow those of prompts 0 to p - 1. The counts sum to 128, and some prompt has exactly 21 rows.
All inputs are finite; a program needn't handle non-finite values.
Results may differ from a plain program's by a relative error of at most 0.023.
The roundings to bfloat16 on the way count: a program that leaves them out, or rounds other values in their place, can miss the bound.
Values may be sent and summed in bfloat16 or wider, within the bound.
No kernel may reach another device: no remote copies, remote signals or barrier semaphores. Data moves between devices by JAX's collectives and lax.ppermute only.
A program may use at most 128 MiB of HBM per device.

v0:
```python
import functools
import math

import jax
import jax.numpy as jnp
from jax import lax
from jax.experimental import pallas as pl
from jax.experimental.pallas import tpu as pltpu
from jax.sharding import PartitionSpec as P

PREFIX = 2048
PROM_DEV = 6
PCAP = 21
CHUNK = 7
CHUNKS = PCAP // CHUNK
CORES = 2
SIDE = 2
F32 = jnp.float32
BF16 = jnp.bfloat16


def room(mib):
    return pltpu.CompilerParams(vmem_limit_bytes=mib << 20)


def vmem():
    return pl.BlockSpec(memory_space=pltpu.VMEM)


def norm_kernel(x_ref, gain_ref, near_ref, far_ref):
    x = x_ref[...].astype(F32)
    inverse = lax.rsqrt(jnp.mean(x * x, axis=1, keepdims=True) + 1e-05)
    value = (x * inverse * gain_ref[...].astype(F32)[None, :]).astype(BF16)
    cut = near_ref.shape[1]
    near_ref[...] = value[:, :cut]
    far_ref[...] = value[:, cut:]


def norm_rows(hidden, gain, cut):
    rows, cols = hidden.shape
    return pl.pallas_call(
        norm_kernel,
        out_shape=(
            jax.ShapeDtypeStruct((rows, cut), BF16),
            jax.ShapeDtypeStruct((rows, cols - cut), BF16),
        ),
        in_specs=[vmem(), vmem()],
        out_specs=(vmem(), vmem()),
        compiler_params=room(4),
    )(hidden, gain)


def place(me):
    core = lax.rem(me, CORES)
    side = lax.rem(lax.div(me, CORES), SIDE)
    return core, side


ORDER = ((0, 0), (1, 0), (0, 1), (1, 1))


def joined(pieces, start, size):
    columns = pl.ds(pl.multiple_of(start, size), size)
    return jnp.concatenate([p[:, columns] for p in pieces], axis=0)


def settle(scratch, value, me):
    core, side = place(me)
    rows_z = value.shape[0] // 4
    for k, (ds_, dc) in enumerate(ORDER):
        part = value[k * rows_z : (k + 1) * rows_z]
        scratch[:, side ^ ds_, core ^ dc] = part.reshape(rows_z // 8, 8, part.shape[1])


def kv_kernel(cut, a0, a1, a2, a3, b0, b1, wkv_ref, keep_ref, send_ref, kv_sc, x_sc):
    me = lax.axis_index("tensor")
    slab = wkv_ref.shape[0]
    heads = wkv_ref.shape[1] // (2 * 128)
    width = 2 * 128
    head = lax.rem(me, heads)
    first = me * slab

    @pl.when(first < cut)
    def _():
        x_sc[...] = joined((a0, a1, a2, a3), first, slab)

    @pl.when(first >= cut)
    def _():
        x_sc[...] = joined((b0, b1), first - cut, slab)

    x = x_sc[...]
    for j in range(heads):
        col = pl.multiple_of((head ^ j) * width, width)
        part = jnp.dot(x, wkv_ref[:, pl.ds(col, width)], preferred_element_type=F32)
        settle(kv_sc.at[j], part, me)
        value = kv_sc[j].reshape(part.shape)
        half = (j // 2) * width
        if j % 2:
            send_ref[:, half : half + width] = value.astype(BF16)
        else:
            keep_ref[:, half : half + width] = value


def project_kv(near, far, wkv):
    rows_z, cut = near[0].shape
    rows = 4 * rows_z
    slab, kv_cols = wkv.shape
    heads = kv_cols // 256
    return pl.pallas_call(
        functools.partial(kv_kernel, cut),
        out_shape=(
            jax.ShapeDtypeStruct((rows, kv_cols // 2), F32),
            jax.ShapeDtypeStruct((rows, kv_cols // 2), BF16),
        ),
        in_specs=[vmem()] * 7,
        out_specs=(vmem(), vmem()),
        scratch_shapes=[
            pltpu.VMEM((heads, rows_z // 8, SIDE, CORES, 8, 256), F32),
            pltpu.VMEM((rows, slab), BF16),
        ],
        compiler_params=room(14),
        cost_estimate=pl.CostEstimate(
            flops=2 * rows * slab * kv_cols,
            bytes_accessed=2 * (slab * kv_cols + 4 * rows * cut),
            transcendentals=0,
        ),
    )(*near, *far, wkv)


def near_kernel(a0, a1, a2, a3, wq_ref, out_ref):
    step = pl.program_id(0)
    block = wq_ref.shape[0]
    x = joined((a0, a1, a2, a3), step * block, block)
    value = jnp.dot(x, wq_ref[...], preferred_element_type=F32)

    @pl.when(step == 0)
    def _():
        out_ref[...] = value

    @pl.when(step > 0)
    def _():
        out_ref[...] += value


def far_kernel(b0, b1, wq_ref, acc_ref, out_ref, acc, q_sc):
    step = pl.program_id(0)
    block = wq_ref.shape[0]

    @pl.when(step == 0)
    def _():
        acc[...] = acc_ref[...]

    acc[...] += jnp.dot(
        joined((b0, b1), step * block, block), wq_ref[...], preferred_element_type=F32
    )

    @pl.when(step == pl.num_programs(0) - 1)
    def _():
        settle(q_sc, acc[...], lax.axis_index("tensor"))
        out_ref[...] = q_sc[...].reshape(out_ref.shape).astype(BF16)


def whole(shape):
    return pl.BlockSpec(shape, lambda i: (0, 0))


def product_cost(rows, share, cols):
    return pl.CostEstimate(
        flops=2 * rows * share * cols,
        bytes_accessed=2 * share * (cols + rows),
        transcendentals=0,
    )


def query_near(near, wq, block=1024):
    rows_z, cut = near[0].shape
    rows, cols = 4 * rows_z, wq.shape[1]
    return pl.pallas_call(
        near_kernel,
        grid=(cut // block,),
        out_shape=jax.ShapeDtypeStruct((rows, cols), F32),
        in_specs=[whole(p.shape) for p in near] + [pl.BlockSpec((block, cols), lambda i: (i, 0))],
        out_specs=whole((rows, cols)),
        compiler_params=room(12),
        cost_estimate=product_cost(rows, cut, cols),
    )(*near, wq)


def query_far(far, wq, half, block=1024):
    rows, cols = half.shape
    share = far[0].shape[1]
    return pl.pallas_call(
        far_kernel,
        grid=(share // block,),
        out_shape=jax.ShapeDtypeStruct((rows, cols), BF16),
        in_specs=[whole(p.shape) for p in far]
        + [pl.BlockSpec((block, cols), lambda i: (i, 0)), whole((rows, cols))],
        out_specs=whole((rows, cols)),
        scratch_shapes=[
            pltpu.VMEM((rows, cols), F32),
            pltpu.VMEM((rows // (8 * CORES * SIDE), SIDE, CORES, 8, cols), F32),
        ],
        compiler_params=room(12),
        cost_estimate=product_cost(rows, share, cols),
    )(*far, wq, half)


def trips(work, cap):
    for b in range(cap // CHUNK):
        work(b, 0)


def attend_kernel(
    groups, kvh, hs, counts_ref, lens_ref, *refs
):
    q_in = refs[:groups]
    kv_ref, cos_ref, sin_ref, pk_ref, pv_ref, sk_ref, sv_ref = refs[groups : groups + 7]
    outs = refs[groups + 7 : 2 * groups + 7]
    q_sc, k_sc, v_sc, o_sc, ss_sc, sp_sc, ac_sc, key_buf, value_buf, sems = refs[2 * groups + 7 :]
    step = pl.program_id(0)
    me = lax.axis_index("tensor")
    group = lax.div(me, kvh)
    rows = cos_ref.shape[0]
    hd = cos_ref.shape[1]
    heads = groups * hs
    smax = sk_ref.shape[2]
    scaling = 1.0 / math.sqrt(hd)

    def rope(x, cosines, sines):
        return x * cosines + pltpu.roll(x, hd // 2, 1) * sines

    def rounded(x):
        return x.astype(BF16).astype(F32)

    def fetch(p, c, kind):
        source, target = ((sk_ref, key_buf), (sv_ref, value_buf))[kind]
        span = pl.ds(p * PCAP + c * CHUNK, CHUNK)
        return pltpu.make_async_copy(
            source.at[0, span], target.at[span], sems.at[kind, p * CHUNKS + c]
        )

    @pl.when(step == 0)
    def _():
        for p in range(PROM_DEV):
            held = counts_ref[group * PROM_DEV + p]
            for c in range(CHUNKS):

                @pl.when(held > c * CHUNK)
                def _(p=p, c=c):
                    fetch(p, c, 0).start()
                    fetch(p, c, 1).start()

        cosines, sines = cos_ref[...], sin_ref[...]
        q_sc[pl.ds(rows, PCAP + 3)] = jnp.zeros((PCAP + 3, heads, hd), F32)
        k_sc[pl.ds(rows, PCAP + 3)] = jnp.zeros((PCAP + 3, heads, hd), F32)
        v_sc[pl.ds(rows, PCAP + 3)] = jnp.zeros((PCAP + 3, heads, hd), F32)
        o_sc[...] = jnp.zeros_like(o_sc)
        for s in range(groups):
            which = lax.rem(group - s + groups, groups)
            for j in range(hs):
                cols = slice(j * hd, (j + 1) * hd)
                x = q_in[0][:, cols]
                for k in range(1, groups):
                    x = jnp.where(which == k, q_in[k][:, cols], x)
                q_sc[pl.ds(0, rows), s * hs + j] = rounded(rope(x.astype(F32), cosines, sines))
        key = rounded(rope(rounded(kv_ref[:, :hd]), cosines, sines))
        value = rounded(kv_ref[:, hd:])
        for j in range(heads):
            k_sc[pl.ds(0, rows), j] = key
            v_sc[pl.ds(0, rows), j] = value

    prompt = group * PROM_DEV + step
    start = lax.fori_loop(0, prompt, lambda p, t: t + counts_ref[p], 0)
    count = counts_ref[prompt]
    contract = (((1,), (1,)), ((), ()))
    token = lax.broadcasted_iota(jnp.int32, (heads, smax), 1)
    base = step * PCAP

    def prompt_rows(cap):
        flat = cap * heads
        q_wide = q_sc[pl.ds(start, cap)].reshape(flat, hd)
        k_wide = k_sc[pl.ds(start, cap)].reshape(flat, hd)
        own = jnp.sum(q_wide * k_wide, axis=1, keepdims=True) * scaling
        scores = (
            lax.dot_general(
                q_wide.astype(BF16), pk_ref[0, 0], contract, preferred_element_type=F32
            )
            * scaling
        )

        def score_rows(b, carry):
            for u in range(CHUNK):
                r = b * CHUNK + u
                at = jnp.minimum(start + r, rows - 1)
                row_q = q_sc[start + r].astype(BF16)
                value = (
                    lax.dot_general(row_q, key_buf[base + r], contract, preferred_element_type=F32)
                    * scaling
                )
                ss_sc[r] = jnp.where(token < lens_ref[at], value, -jnp.inf)
            return carry

        for c in range(cap // CHUNK):
            fetch(step, c, 0).wait()
        trips(score_rows, cap)
        tail = ss_sc[:cap].reshape(flat, smax)
        highest = jnp.maximum(
            jnp.max(scores, axis=1, keepdims=True),
            jnp.maximum(jnp.max(tail, axis=1, keepdims=True), own),
        )
        past_exp = jnp.exp(scores - highest)
        tail_exp = jnp.exp(tail - highest)
        own_exp = jnp.exp(own - highest)
        total = (
            jnp.sum(past_exp, axis=1, keepdims=True)
            + jnp.sum(tail_exp, axis=1, keepdims=True)
            + own_exp
        )
        inverse = 1.0 / total
        sp_sc[:cap] = (tail_exp * inverse).reshape(cap, heads, smax)
        past_weights = (past_exp * inverse).astype(BF16)
        own_weight = rounded(own_exp * inverse)
        result = jnp.dot(past_weights, pv_ref[0, 0], preferred_element_type=F32)

        def mix_rows(b, carry):
            for u in range(CHUNK):
                r = b * CHUNK + u
                ac_sc[r] = jnp.dot(
                    sp_sc[r].astype(BF16), value_buf[base + r], preferred_element_type=F32
                )
            return carry

        for c in range(cap // CHUNK):
            fetch(step, c, 1).wait()
        trips(mix_rows, cap)
        result = (
            result
            + ac_sc[:cap].reshape(flat, hd)
            + own_weight * v_sc[pl.ds(start, cap)].reshape(flat, hd)
        )
        slot = lax.broadcasted_iota(jnp.int32, (cap, heads, hd), 0)
        o_sc[pl.ds(start, cap)] = jnp.where(slot < count, result.reshape(cap, heads, hd), 0.0)

    for c in range(CHUNKS):

        @pl.when((count > c * CHUNK) & (count <= (c + 1) * CHUNK))
        def _(c=c):
            prompt_rows((c + 1) * CHUNK)

    @pl.when(step == pl.num_programs(0) - 1)
    def _():
        for k in range(groups):
            which = lax.rem(group - k + groups, groups)
            for j in range(hs):
                x = o_sc[pl.ds(0, rows), j]
                for s in range(1, groups):
                    x = jnp.where(which == s, o_sc[pl.ds(0, rows), s * hs + j], x)
                outs[k][:, j * hd : (j + 1) * hd] = x.astype(BF16)


def attend(groups, kvh, counts, lengths, queries, kv, cosines, sines, pk, pv, sk, sv):
    rows, share = queries[0].shape
    hd = cosines.shape[1]
    hs = share // hd
    heads = groups * hs
    pads = rows + PCAP + 3
    smax = sk.shape[2]
    const = lambda shape: pl.BlockSpec(shape, lambda i, *_: (0,) * len(shape))
    piece = lambda a, n: pl.BlockSpec((1, n) + a.shape[2:], lambda i, *_: (0, i, 0, 0))
    return pl.pallas_call(
        functools.partial(attend_kernel, groups, kvh, hs),
        out_shape=tuple(jax.ShapeDtypeStruct((rows, share), BF16) for _ in range(groups)),
        grid_spec=pltpu.PrefetchScalarGridSpec(
            num_scalar_prefetch=2,
            grid=(PROM_DEV,),
            in_specs=[const(q.shape) for q in queries]
            + [const(kv.shape), const(cosines.shape), const(sines.shape)]
            + [piece(pk, 1), piece(pv, 1)]
            + [pl.BlockSpec(memory_space=pltpu.HBM)] * 2,
            out_specs=tuple(const((rows, share)) for _ in range(groups)),
            scratch_shapes=[pltpu.VMEM((pads, heads, hd), F32)] * 4
            + [
                pltpu.VMEM((PCAP, heads, smax), F32),
                pltpu.VMEM((PCAP, heads, smax), F32),
                pltpu.VMEM((PCAP, heads, hd), F32),
                pltpu.VMEM(sk.shape[1:], BF16),
                pltpu.VMEM(sv.shape[1:], BF16),
                pltpu.SemaphoreType.DMA((2, PROM_DEV * CHUNKS)),
            ],
        ),
        compiler_params=room(41),
        cost_estimate=pl.CostEstimate(
            flops=4 * PROM_DEV * PCAP * heads * hd * (PREFIX + smax),
            bytes_accessed=2 * (pk.size + pv.size + sk.size + sv.size),
            transcendentals=PROM_DEV * PCAP * heads * (PREFIX + smax),
        ),
    )(counts, lengths, *queries, kv, cosines, sines, pk, pv, sk, sv)


def output_kernel(groups, zn, *refs):
    parts = refs[:groups]
    w_ref, keep_ref, send_ref, a_sc, r_sc, x_sc = refs[groups:]
    step = pl.program_id(0)
    rows = x_sc.shape[0]
    half = rows // 2

    @pl.when(step == 0)
    def _():
        me = lax.axis_index("tensor")
        core, side = place(me)
        depth = lax.div(me, CORES * SIDE)
        total = parts[0][...].astype(F32)
        for p in parts[1:]:
            total = total + p[...].astype(F32)
        a_sc[...] = total.reshape(a_sc.shape)
        for dc in range(CORES):
            for ds_ in range(SIDE):
                for k in range(zn):
                    z = lax.rem(depth + k, zn)
                    r_sc[dc, ds_, k] = a_sc[z, side ^ ds_, core ^ dc]
        x_sc[...] = r_sc[...].reshape(x_sc.shape).astype(BF16)

    value = jnp.dot(x_sc[...], w_ref[...], preferred_element_type=F32).astype(BF16)
    keep_ref[...] = value[:half]
    send_ref[...] = value[half:]


def output_product(parts, w):
    groups = len(parts)
    rows, share = parts[0].shape
    cols = w.shape[1]
    block = 1024
    zn = rows // (8 * CORES * SIDE)
    half = rows // 2
    return pl.pallas_call(
        functools.partial(output_kernel, groups, zn),
        grid=(cols // block,),
        out_shape=(jax.ShapeDtypeStruct((half, cols), BF16),) * 2,
        in_specs=[pl.BlockSpec((rows, share), lambda i: (0, 0)) for _ in parts]
        + [pl.BlockSpec((share, block), lambda i: (0, i))],
        out_specs=(pl.BlockSpec((half, block), lambda i: (0, i)),) * 2,
        scratch_shapes=[
            pltpu.VMEM((zn, SIDE, CORES, 8, share), F32),
            pltpu.VMEM((CORES, SIDE, zn, 8, share), F32),
            pltpu.VMEM((rows, share), BF16),
        ],
        compiler_params=room(10),
        cost_estimate=pl.CostEstimate(
            flops=2 * rows * share * cols,
            bytes_accessed=2 * (share * cols + rows * cols),
            transcendentals=0,
        ),
    )(*parts, w)


def local(
    hidden_in,
    norm_gain,
    w_query,
    w_kv,
    w_out,
    prefix_keys,
    prefix_values,
    suffix_keys,
    suffix_values,
    row_counts,
    suffix_lengths,
):
    devices = lax.axis_size("tensor")
    me = lax.axis_index("tensor")
    kvh = w_kv.shape[1]
    hd = w_query.shape[2]
    hs = w_query.shape[1]
    slab = w_kv.shape[0]
    groups = devices // kvh
    line = CORES * SIDE
    zn = devices // line
    depth = me // line

    def move(x, pairs):
        return lax.ppermute(x, "tensor", pairs)

    def swap(x, bit):
        return move(x, [(i, i ^ bit) for i in range(devices)])

    def shift(x, k):
        return move(x, [(i, (i + k * line) % devices) for i in range(devices)])

    wkv = w_kv.reshape(slab, kvh * 2 * hd)
    frequency = 500000.0 ** (-(2.0 * jnp.arange(hd // 2, dtype=F32)) / hd)
    angle = (PREFIX + suffix_lengths).astype(F32)[:, None] * frequency[None, :]
    cos_half, sin_half = jnp.cos(angle), jnp.sin(angle)
    cosines = jnp.concatenate([cos_half, cos_half], axis=1)
    sines = jnp.concatenate([-sin_half, sin_half], axis=1)

    width_all = hidden_in.shape[1]
    local_rows = hidden_in.shape[0]
    cut = width_all // 8 * 5
    near, far = norm_rows(hidden_in, norm_gain, cut)
    near_moved = [near] + [shift(near, k) for k in range(1, zn)]
    far_pair = jnp.stack([far, swap(far, CORES)])
    near_rows = jnp.zeros((zn,) + near.shape, BF16)
    for k in range(zn):
        near_rows = lax.dynamic_update_index_in_dim(
            near_rows, near_moved[k], lax.rem(depth - k + zn, zn), 0
        )
    near_rows, far_pair, wkv, w_query = lax.optimization_barrier(
        (near_rows, far_pair, wkv, w_query)
    )
    wq_near = w_query[:cut].reshape(cut, hs * hd)
    wq_far = w_query[cut:].reshape(width_all - cut, hs * hd)
    near_mine = near_rows.reshape(zn * local_rows, cut)
    near_across = swap(near_mine, CORES)
    far_rows = jnp.zeros((SIDE, zn) + far.shape, BF16)
    for k in range(zn):
        moved = far_pair if k == 0 else shift(far_pair, k)
        far_rows = lax.dynamic_update_index_in_dim(
            far_rows, moved, lax.rem(depth - k + zn, zn), 1
        )
    far_mine = far_rows.reshape(SIDE * zn * local_rows, width_all - cut)
    near_mine_next = swap(near_mine, 1)
    near_across, far_mine, wq_near, wq_far, cosines, sines = lax.optimization_barrier(
        (near_across, far_mine, wq_near, wq_far, cosines, sines)
    )
    near_pieces = [near_mine, near_across, near_mine_next, swap(near_across, 1)]
    far_pieces = [far_mine, swap(far_mine, 1)]

    keep, send = project_kv(near_pieces, far_pieces, wkv)
    came = swap(send, 1)
    near_pieces[0], keep = lax.optimization_barrier((near_pieces[0], keep))
    half = query_near(near_pieces, wq_near)
    width = 2 * hd

    def blocks(x, first):
        return jnp.concatenate(
            [x[:, b * width : (b + 1) * width] for b in range(first, x.shape[1] // width, 2)], 1
        )

    came, half = lax.optimization_barrier((came, half))
    total = keep + came.astype(F32)
    came = swap(blocks(total, 1).astype(BF16), CORES)
    query = query_far(far_pieces, wq_far, half)
    came, query = lax.optimization_barrier((came, query))
    total = blocks(total, 0) + came.astype(F32)
    received = [
        move(query, [(i, ((i % groups + k) % groups) * kvh + i // groups) for i in range(devices)])
        for k in range(groups)
    ]
    bit = CORES
    while bit * 2 < devices:
        bit *= 2
        if bit < kvh:
            total = blocks(total, 0) + swap(blocks(total, 1).astype(BF16), bit).astype(F32)
        else:
            sent = total.astype(BF16)
            total = total + swap(sent, bit).astype(F32)

    attended = attend(
        groups,
        kvh,
        row_counts,
        suffix_lengths,
        received,
        total,
        cosines,
        sines,
        prefix_keys,
        prefix_values,
        suffix_keys,
        suffix_values,
    )
    parts = [
        move(
            attended[k],
            [(((i % groups + k) % groups) * kvh + i // groups, i) for i in range(devices)],
        )
        for k in range(groups)
    ]
    keep, send = output_product(parts, w_out.reshape(hs * hd, w_out.shape[2]))
    came = swap(send, 1)
    part = zn * local_rows

    def pair_sum(first, last):
        return (keep[first[0] : first[1], last].astype(F32) + came[first[0] : first[1], last].astype(F32))

    own, other = (0, part), (part, 2 * part)
    near_cols, far_cols = slice(0, cut), slice(cut, width_all)
    near_go = swap(pair_sum(other, near_cols).astype(BF16), CORES)
    far_all = jnp.concatenate([pair_sum(own, far_cols), pair_sum(other, far_cols)], 0)
    far_all = far_all.astype(BF16).reshape(SIDE, zn, local_rows, width_all - cut)
    far_moved = [shift(far_all[:, k], k) for k in range(1, zn)]
    near_sum = pair_sum(own, near_cols).astype(BF16).astype(F32) + near_go.astype(F32)
    near_all = near_sum.astype(BF16).reshape(zn, local_rows, cut)
    near_moved = [shift(near_all[k], k) for k in range(1, zn)]
    far_sum = far_all[:, 0].astype(F32)
    for moved in far_moved:
        far_sum = far_sum + moved.astype(F32)
    far_back = swap(far_sum[1].astype(BF16), CORES)
    near_sum = near_all[0].astype(F32)
    for moved in near_moved:
        near_sum = near_sum + moved.astype(F32)
    far_sum = far_sum[0] + far_back.astype(F32)
    summed = jnp.concatenate([near_sum, far_sum], axis=1)
    return (hidden_in.astype(F32) + summed).astype(BF16)


def solution(mesh):
    in_specs = (
        P(("groups", "tensor"), None),
        P(),
        P(None, "tensor", None),
        P("tensor", None, None, None),
        P("tensor", None, None),
        P(("groups", "tensor"), None, None, None),
        P(("groups", "tensor"), None, None, None),
        P(("groups", "tensor"), None, None, None),
        P(("groups", "tensor"), None, None, None),
        P("groups"),
        P("groups"),
    )
    out_specs = P(("groups", "tensor"), None)
    return jax.shard_map(local, mesh=mesh, in_specs=in_specs, out_specs=out_specs, check_vma=False)
```

profile of v0, /device:TPU:0, one launch (start us, length us, event | category | flops | bytes accessed | tf_op | source)
XLA Modules:
  0.0 109.8 jit_solution(8840142977819902174)
XLA Ops:
  0.0 0.9 copy-done.2
  0.9 0.7 copy-done.4
  1.6 0.2 shard_map.109
  1.8 3.1 %collective-permute-start = (bf16[8,5120]{1,0:T(8,128)(2,1)S(1)}, bf16[8,5120]{1,0:T(8,128)(2,1)S(1)}, u32[]{:S(2)}, u32[]{:S(2)}) collective-permute-start(bf16[8,5120]{1,0:T(8,128)(2,1)S(1)} %get-tuple-element.29), channel_id=1, source_target_pairs={{0,4},{1,5},{2,6},{3,7},{4,8},{5,9},{6,10},{7,11},{8,12},{9,13},{1... | collective-permute-start | bytes 245768 | tf_op jit(solution)/shard_map/ppermute | solution.py:481
  4.9 2.6 %collective-permute-start.1 = (bf16[8,5120]{1,0:T(8,128)(2,1)S(1)}, bf16[8,5120]{1,0:T(8,128)(2,1)S(1)}, u32[]{:S(2)}, u32[]{:S(2)}) collective-permute-start(bf16[8,5120]{1,0:T(8,128)(2,1)S(1)} %get-tuple-element.29), channel_id=1, source_target_pairs={{0,8},{1,9},{2,10},{3,11},{4,12},{5,13},{6,14},{7,15},{8,0},{9,1},... | collective-permute-start | bytes 245768 | tf_op jit(solution)/shard_map/ppermute | solution.py:481
  7.5 1.3 %collective-permute-start.2 = (bf16[8,5120]{1,0:T(8,128)(2,1)S(1)}, bf16[8,5120]{1,0:T(8,128)(2,1)S(1)}, u32[]{:S(2)}, u32[]{:S(2)}) collective-permute-start(bf16[8,5120]{1,0:T(8,128)(2,1)S(1)} %get-tuple-element.29), channel_id=1, source_target_pairs={{0,12},{1,13},{2,14},{3,15},{4,0},{5,1},{6,2},{7,3},{8,4},{9,5},{1... | collective-permute-start | bytes 245768 | tf_op jit(solution)/shard_map/ppermute | solution.py:481
  8.9 1.5 %collective-permute-start.3 = (bf16[8,3072]{1,0:T(8,128)(2,1)S(1)}, bf16[8,3072]{1,0:T(8,128)(2,1)S(1)}, u32[]{:S(2)}, u32[]{:S(2)}) collective-permute-start(bf16[8,3072]{1,0:T(8,128)(2,1)S(1)} %get-tuple-element.30), channel_id=1, source_target_pairs={{0,2},{1,3},{2,0},{3,1},{4,6},{5,7},{6,4},{7,5},{8,10},{9,11},{10,... | collective-permute-start | bytes 147464 | tf_op jit(solution)/shard_map/ppermute | solution.py:481
  10.4 0.7 add_convert_fusion.5
  11.1 0.3 fusion.6
  11.4 0.1 pad_maximum_fusion.3
  11.6 3.3 %reshape.41.wkv_ref = bf16[512,2048]{1,0:T(8,128)(2,1)S(1)} reshape(bf16[512,8,2,128]{3,2,1,0:T(2,128)(2,1)} %param.14) | data formatting | bytes 4194304 | tf_op jit(solution)/shard_map/reshape | solution.py:489
  15.0 0.7 collective-permute-start.5
  15.8 0.0 slice-start.2
  15.8 1.5 %collective-permute-start.6 = (bf16[2,8,3072]{2,1,0:T(8,128)(2,1)S(1)}, bf16[2,8,3072]{2,1,0:T(8,128)(2,1)S(1)}, u32[]{:S(2)}, u32[]{:S(2)}) collective-permute-start(bf16[2,8,3072]{2,1,0:T(8,128)(2,1)S(1)} %pad_maximum_fusion.2), channel_id=1, source_target_pairs={{0,8},{1,9},{2,10},{3,11},{4,12},{5,13},{6,14},{7,15},{8,0},{9,1},... | collective-permute-start | bytes 294920 | tf_op jit(solution)/shard_map/ppermute | solution.py:481
  17.3 1.8 %collective-permute-start.7 = (bf16[2,8,3072]{2,1,0:T(8,128)(2,1)S(1)}, bf16[2,8,3072]{2,1,0:T(8,128)(2,1)S(1)}, u32[]{:S(2)}, u32[]{:S(2)}) collective-permute-start(bf16[2,8,3072]{2,1,0:T(8,128)(2,1)S(1)} %pad_maximum_fusion.2), channel_id=1, source_target_pairs={{0,12},{1,13},{2,14},{3,15},{4,0},{5,1},{6,2},{7,3},{8,4},{9,5},{1... | collective-permute-start | bytes 294920 | tf_op jit(solution)/shard_map/ppermute | solution.py:481
  19.1 0.9 copy.28
  20.0 1.0 slice-done.3
  21.0 0.5 copy.29
  21.5 0.6 collective-permute-start.4
  22.1 0.4 collective-permute-done.5
  22.5 2.1 %collective-permute-done.6 = bf16[2,8,3072]{2,1,0:T(8,128)(2,1)S(1)} collective-permute-done((bf16[2,8,3072]{2,1,0:T(8,128)(2,1)S(1)}, bf16[2,8,3072]{2,1,0:T(8,128)(2,1)S(1)}, u32[]{:S(2)}, u32[]{:S(2)}) %collective-permute-start.6) | collective-permute-done | bytes 98336 | tf_op jit(solution)/shard_map/ppermute | solution.py:481
  24.6 5.1 %collective-permute-done.4.a1 = bf16[32,5120]{1,0:T(8,128)(2,1)S(1)} collective-permute-done((bf16[32,5120]{1,0:T(8,128)(2,1)S(1)}, bf16[32,5120]{1,0:T(8,128)(2,1)S(1)}, u32[]{:S(2)}, u32[]{:S(2)}) %collective-permute-start.4) | collective-permute-done | bytes 327712 | tf_op jit(solution)/shard_map/ppermute | solution.py:481
  29.7 0.5 collective-permute-start.8
  30.2 1.7 %collective-permute-done.8.a2 = bf16[32,5120]{1,0:T(8,128)(2,1)S(1)} collective-permute-done((bf16[32,5120]{1,0:T(8,128)(2,1)S(1)}, bf16[32,5120]{1,0:T(8,128)(2,1)S(1)}, u32[]{:S(2)}, u32[]{:S(2)}) %collective-permute-start.8) | collective-permute-done | bytes 327712 | tf_op jit(solution)/shard_map/ppermute | solution.py:481
  31.9 0.5 collective-permute-done.9.a3
  32.3 0.5 shard_map.110
  32.9 0.2 collective-permute-start.11
  33.1 1.7 %shard_map.111.acc_ref = f32[128,512]{1,0:T(8,128)S(1)} custom-call(bf16[32,5120]{1,0:T(8,128)(2,1)S(1)} %bitcast.74, bf16[32,5120]{1,0:T(8,128)(2,1)S(1)} %collective-permute-done.4.a1, bf16[32,5120]{1,0:T(8,128)(2,1)S(1)} %collective-permute-done.8.a2, bf16[32,5120]{1,0:T(8,128)(2,1)S(1)} %collective-permute-done.9.a3, bf16[5120,512]{1,0:T(8,128)(2,1)S(1)} %bitcast.63), custom_call_target="tpu_custom_call" | custom-call | flops 671088640 | bytes 6553600 | tf_op jit(solution)/shard_map/pallas_call | solution.py:178
  34.8 0.0 copy-start
  34.8 0.0 copy-start.6
  34.9 0.1 fusion.7
  35.0 1.5 %collective-permute-start.12 = (bf16[128,512]{1,0:T(8,128)(2,1)S(1)}, bf16[128,512]{1,0:T(8,128)(2,1)S(1)}, u32[]{:S(2)}, u32[]{:S(2)}) collective-permute-start(bf16[128,512]{1,0:T(8,128)(2,1)S(1)} %pad_maximum_fusion.1), channel_id=1, source_target_pairs={{0,2},{1,3},{2,0},{3,1},{4,6},{5,7},{6,4},{7,5},{8,10},{9,11},{10,... | collective-permute-start | bytes 393224 | tf_op jit(solution)/shard_map/ppermute | solution.py:481
  36.5 1.1 shard_map.112
  37.5 3.3 %collective-permute-done.12 = bf16[128,512]{1,0:T(8,128)(2,1)S(1)} collective-permute-done((bf16[128,512]{1,0:T(8,128)(2,1)S(1)}, bf16[128,512]{1,0:T(8,128)(2,1)S(1)}, u32[]{:S(2)}, u32[]{:S(2)}) %collective-permute-start.12) | collective-permute-done | bytes 131104 | tf_op jit(solution)/shard_map/ppermute | solution.py:481
  40.9 0.4 collective-permute-start.15
  41.2 4.0 %collective-permute-done.15 = bf16[128,256]{1,0:T(8,128)(2,1)S(1)} collective-permute-done((bf16[128,256]{1,0:T(8,128)(2,1)S(1)}, bf16[128,256]{1,0:T(8,128)(2,1)S(1)}, u32[]{:S(2)}, u32[]{:S(2)}) %collective-permute-start.15) | collective-permute-done | bytes 65568 | tf_op jit(solution)/shard_map/ppermute | solution.py:481
  45.2 1.4 %collective-permute-start.16 = (bf16[128,256]{1,0:T(8,128)(2,1)S(1)}, bf16[128,256]{1,0:T(8,128)(2,1)S(1)}, u32[]{:S(2)}, u32[]{:S(2)}) collective-permute-start(bf16[128,256]{1,0:T(8,128)(2,1)S(1)} %fusion.4), channel_id=1, source_target_pairs={{0,8},{1,9},{2,10},{3,11},{4,12},{5,13},{6,14},{7,15},{8,0},{9,1},... | collective-permute-start | bytes 196616 | tf_op jit(solution)/shard_map/ppermute | solution.py:481
  46.7 0.7 collective-permute-start.13
  47.3 4.3 %collective-permute-start.14 = (bf16[128,512]{1,0:T(8,128)(2,1)S(1)}, bf16[128,512]{1,0:T(8,128)(2,1)S(1)}, u32[]{:S(2)}, u32[]{:S(2)}) collective-permute-start(bf16[128,512]{1,0:T(8,128)(2,1)S(1)} %shard_map.112), channel_id=1, source_target_pairs={{0,8},{1,0},{2,9},{3,1},{4,10},{5,2},{6,11},{7,3},{8,12},{9,4},{10... | collective-permute-start | bytes 393224 | tf_op jit(solution)/shard_map/ppermute | solution.py:481
  51.6 0.0 slice-start.1
  51.6 2.5 %collective-permute-done.14.refs_1_ = bf16[128,512]{1,0:T(8,128)(2,1)S(1)} collective-permute-done((bf16[128,512]{1,0:T(8,128)(2,1)S(1)}, bf16[128,512]{1,0:T(8,128)(2,1)S(1)}, u32[]{:S(2)}, u32[]{:S(2)}) %collective-permute-start.14) | collective-permute-done | bytes 131104 | tf_op jit(solution)/shard_map/ppermute | solution.py:481
  54.1 11.9 %shard_map.113 = (bf16[128,512]{1,0:T(8,128)(2,1)S(1)}, bf16[128,512]{1,0:T(8,128)(2,1)S(1)}) custom-call(s32[12]{0:T(128)S(1)} %copy-done.5, s32[128]{0:T(128)S(1)} %copy-done.6, bf16[128,512]{1,0:T(8,128)(2,1)S(1)} %collective-permute-done.13.refs_0_, bf16[128,512]{1,0:T(8,128)(2,1)S(1)} %collective-permute-done.14.refs_1_, ...), custom_call_target="tpu_custom_call" | custom-call | flops 1189085184 | bytes 22806528 | tf_op jit(solution)/shard_map/pallas_call | solution.py:370
  66.0 0.7 collective-permute-start.17
  66.7 4.0 %collective-permute-start.18 = (bf16[128,512]{1,0:T(8,128)(2,1)S(1)}, bf16[128,512]{1,0:T(8,128)(2,1)S(1)}, u32[]{:S(2)}, u32[]{:S(2)}) collective-permute-start(bf16[128,512]{1,0:T(8,128)(2,1)S(1)} %get-tuple-element.50), channel_id=1, source_target_pairs={{8,0},{0,1},{9,2},{1,3},{10,4},{2,5},{11,6},{3,7},{12,8},{4,9},{13... | collective-permute-start | bytes 393224 | tf_op jit(solution)/shard_map/ppermute | solution.py:481
  70.7 5.9 %collective-permute-done.18.refs_1_ = bf16[128,512]{1,0:T(8,128)(2,1)S(1)} collective-permute-done((bf16[128,512]{1,0:T(8,128)(2,1)S(1)}, bf16[128,512]{1,0:T(8,128)(2,1)S(1)}, u32[]{:S(2)}, u32[]{:S(2)}) %collective-permute-start.18) | collective-permute-done | bytes 131104 | tf_op jit(solution)/shard_map/ppermute | solution.py:481
  76.6 3.4 %shard_map.114 = (bf16[64,8192]{1,0:T(8,128)(2,1)S(1)}, bf16[64,8192]{1,0:T(8,128)(2,1)S(1)}) custom-call(bf16[128,512]{1,0:T(8,128)(2,1)S(1)} %collective-permute-done.17.refs_0_, bf16[128,512]{1,0:T(8,128)(2,1)S(1)} %collective-permute-done.18.refs_1_, bf16[512,8192]{1,0:T(8,128)(2,1)S(1)} %bitcast.67), custom_call_target="tpu_custom_call" | custom-call | flops 1073741824 | bytes 10485760 | tf_op jit(solution)/shard_map/pallas_call | solution.py:435
  80.1 0.0 copy-start.3
  80.1 0.1 collective-permute-start.19
  80.1 2.6 %collective-permute-done.19 = bf16[64,8192]{1,0:T(8,128)(2,1)S(1)} collective-permute-done((bf16[64,8192]{1,0:T(8,128)(2,1)S(1)}, bf16[64,8192]{1,0:T(8,128)(2,1)S(1)}, u32[]{:S(2)}, u32[]{:S(2)}) %collective-permute-start.19) | collective-permute-done | bytes 1048608 | tf_op jit(solution)/shard_map/ppermute | solution.py:481
  82.8 0.1 add_convert_fusion.4
  83.0 5.2 %collective-permute-start.24 = (bf16[2,8,3072]{2,1,0:T(8,128)(2,1)S(1)}, bf16[2,8,3072]{2,1,0:T(8,128)(2,1)S(1)}, u32[]{:S(2)}, u32[]{:S(2)}) collective-permute-start(bf16[2,8,3072]{2,1,0:T(8,128)(2,1)S(1)} %get-tuple-element.59), channel_id=1, source_target_pairs={{0,4},{1,5},{2,6},{3,7},{4,8},{5,9},{6,10},{7,11},{8,12},{9,13},{1... | collective-permute-start | bytes 294920 | tf_op jit(solution)/shard_map/ppermute | solution.py:481
  88.2 2.4 %collective-permute-start.26 = (bf16[2,8,3072]{2,1,0:T(8,128)(2,1)S(1)}, bf16[2,8,3072]{2,1,0:T(8,128)(2,1)S(1)}, u32[]{:S(2)}, u32[]{:S(2)}) collective-permute-start(bf16[2,8,3072]{2,1,0:T(8,128)(2,1)S(1)} %get-tuple-element.61), channel_id=1, source_target_pairs={{0,12},{1,13},{2,14},{3,15},{4,0},{5,1},{6,2},{7,3},{8,4},{9,5},{1... | collective-permute-start | bytes 294920 | tf_op jit(solution)/shard_map/ppermute | solution.py:481
  90.6 0.1 add_convert_fusion.1
  90.7 1.4 %collective-permute-start.20 = (bf16[32,5120]{1,0:T(8,128)(2,1)S(1)}, bf16[32,5120]{1,0:T(8,128)(2,1)S(1)}, u32[]{:S(2)}, u32[]{:S(2)}) collective-permute-start(bf16[32,5120]{1,0:T(8,128)(2,1)S(1)} %add_convert_fusion.1), channel_id=1, source_target_pairs={{0,2},{1,3},{2,0},{3,1},{4,6},{5,7},{6,4},{7,5},{8,10},{9,11},{10,... | collective-permute-start | bytes 983048 | tf_op jit(solution)/shard_map/ppermute | solution.py:481
  92.0 3.8 %collective-permute-done.25 = bf16[2,8,3072]{2,1,0:T(8,128)(2,1)S(1)} collective-permute-done((bf16[2,8,3072]{2,1,0:T(8,128)(2,1)S(1)}, bf16[2,8,3072]{2,1,0:T(8,128)(2,1)S(1)}, u32[]{:S(2)}, u32[]{:S(2)}) %collective-permute-start.25) | collective-permute-done | bytes 98336 | tf_op jit(solution)/shard_map/ppermute | solution.py:481
  95.9 2.2 %collective-permute-start.27 = (bf16[8,3072]{1,0:T(8,128)(2,1)S(1)}, bf16[8,3072]{1,0:T(8,128)(2,1)S(1)}, u32[]{:S(2)}, u32[]{:S(2)}) collective-permute-start(bf16[8,3072]{1,0:T(8,128)(2,1)S(1)} %fusion.5), channel_id=1, source_target_pairs={{0,2},{1,3},{2,0},{3,1},{4,6},{5,7},{6,4},{7,5},{8,10},{9,11},{10,... | collective-permute-start | bytes 147464 | tf_op jit(solution)/shard_map/ppermute | solution.py:481
  98.2 2.5 %collective-permute-done.20 = bf16[32,5120]{1,0:T(8,128)(2,1)S(1)} collective-permute-done((bf16[32,5120]{1,0:T(8,128)(2,1)S(1)}, bf16[32,5120]{1,0:T(8,128)(2,1)S(1)}, u32[]{:S(2)}, u32[]{:S(2)}) %collective-permute-start.20) | collective-permute-done | bytes 327712 | tf_op jit(solution)/shard_map/ppermute | solution.py:481
  100.7 0.1 add_convert_fusion
  100.9 0.1 collective-permute-start.21
  100.9 1.7 %collective-permute-start.22 = (bf16[8,5120]{1,0:T(8,128)(2,1)S(1)}, bf16[8,5120]{1,0:T(8,128)(2,1)S(1)}, u32[]{:S(2)}, u32[]{:S(2)}) collective-permute-start(bf16[8,5120]{1,0:T(8,128)(2,1)S(1)} %get-tuple-element.64), channel_id=1, source_target_pairs={{0,8},{1,9},{2,10},{3,11},{4,12},{5,13},{6,14},{7,15},{8,0},{9,1},... | collective-permute-start | bytes 245768 | tf_op jit(solution)/shard_map/ppermute | solution.py:481
  102.6 2.1 %collective-permute-start.23 = (bf16[8,5120]{1,0:T(8,128)(2,1)S(1)}, bf16[8,5120]{1,0:T(8,128)(2,1)S(1)}, u32[]{:S(2)}, u32[]{:S(2)}) collective-permute-start(bf16[8,5120]{1,0:T(8,128)(2,1)S(1)} %get-tuple-element.63), channel_id=1, source_target_pairs={{0,12},{1,13},{2,14},{3,15},{4,0},{5,1},{6,2},{7,3},{8,4},{9,5},{1... | collective-permute-start | bytes 245768 | tf_op jit(solution)/shard_map/ppermute | solution.py:481
  104.8 2.6 %collective-permute-done.21 = bf16[8,5120]{1,0:T(8,128)(2,1)S(1)} collective-permute-done((bf16[8,5120]{1,0:T(8,128)(2,1)S(1)}, bf16[8,5120]{1,0:T(8,128)(2,1)S(1)}, u32[]{:S(2)}, u32[]{:S(2)}) %collective-permute-start.21) | collective-permute-done | bytes 81952 | tf_op jit(solution)/shard_map/ppermute | solution.py:481
  107.4 1.7 %collective-permute-done.22 = bf16[8,5120]{1,0:T(8,128)(2,1)S(1)} collective-permute-done((bf16[8,5120]{1,0:T(8,128)(2,1)S(1)}, bf16[8,5120]{1,0:T(8,128)(2,1)S(1)}, u32[]{:S(2)}, u32[]{:S(2)}) %collective-permute-start.22) | collective-permute-done | bytes 81952 | tf_op jit(solution)/shard_map/ppermute | solution.py:481
  109.1 0.7 fusion
  (58 shorter events, 0.5 us)
Async XLA Ops:
  0.0 0.9 copy-start.2
  0.9 0.7 copy-start.4
  1.8 13.1 %collective-permute-start = (bf16[8,5120]{1,0:T(8,128)(2,1)S(1)}, bf16[8,5120]{1,0:T(8,128)(2,1)S(1)}, u32[]{:S(2)}, u32[]{:S(2)}) collective-permute-start(bf16[8,5120]{1,0:T(8,128)(2,1)S(1)} %get-tuple-element.29), channel_id=1, source_target_pairs={{0,4},{1,5},{2,6},{3,7},{4,8},{5,9},{6,10},{7,11},{8,12},{9,13},{1... | collective-permute-start | bytes 245768 | tf_op jit(solution)/shard_map/ppermute | solution.py:481
  4.9 10.0 %collective-permute-start.1 = (bf16[8,5120]{1,0:T(8,128)(2,1)S(1)}, bf16[8,5120]{1,0:T(8,128)(2,1)S(1)}, u32[]{:S(2)}, u32[]{:S(2)}) collective-permute-start(bf16[8,5120]{1,0:T(8,128)(2,1)S(1)} %get-tuple-element.29), channel_id=1, source_target_pairs={{0,8},{1,9},{2,10},{3,11},{4,12},{5,13},{6,14},{7,15},{8,0},{9,1},... | collective-permute-start | bytes 245768 | tf_op jit(solution)/shard_map/ppermute | solution.py:481
  7.5 7.5 %collective-permute-start.2 = (bf16[8,5120]{1,0:T(8,128)(2,1)S(1)}, bf16[8,5120]{1,0:T(8,128)(2,1)S(1)}, u32[]{:S(2)}, u32[]{:S(2)}) collective-permute-start(bf16[8,5120]{1,0:T(8,128)(2,1)S(1)} %get-tuple-element.29), channel_id=1, source_target_pairs={{0,12},{1,13},{2,14},{3,15},{4,0},{5,1},{6,2},{7,3},{8,4},{9,5},{1... | collective-permute-start | bytes 245768 | tf_op jit(solution)/shard_map/ppermute | solution.py:481
  8.9 6.0 %collective-permute-start.3 = (bf16[8,3072]{1,0:T(8,128)(2,1)S(1)}, bf16[8,3072]{1,0:T(8,128)(2,1)S(1)}, u32[]{:S(2)}, u32[]{:S(2)}) collective-permute-start(bf16[8,3072]{1,0:T(8,128)(2,1)S(1)} %get-tuple-element.30), channel_id=1, source_target_pairs={{0,2},{1,3},{2,0},{3,1},{4,6},{5,7},{6,4},{7,5},{8,10},{9,11},{10,... | collective-permute-start | bytes 147464 | tf_op jit(solution)/shard_map/ppermute | solution.py:481
  15.0 7.5 %collective-permute-start.5 = (bf16[2,8,3072]{2,1,0:T(8,128)(2,1)S(1)}, bf16[2,8,3072]{2,1,0:T(8,128)(2,1)S(1)}, u32[]{:S(2)}, u32[]{:S(2)}) collective-permute-start(bf16[2,8,3072]{2,1,0:T(8,128)(2,1)S(1)} %pad_maximum_fusion.2), channel_id=1, source_target_pairs={{0,4},{1,5},{2,6},{3,7},{4,8},{5,9},{6,10},{7,11},{8,12},{9,13},{1... | collective-permute-start | bytes 294920 | tf_op jit(solution)/shard_map/ppermute | solution.py:481
  15.8 3.3 %slice-start.2 = ((bf16[8192,4,128]{2,1,0:T(4,128)(2,1)}), bf16[5120,4,128]{2,1,0:T(4,128)(2,1)S(1)}, s32[]{:S(2)}) async-start(bf16[8192,4,128]{2,1,0:T(4,128)(2,1)} %param.13), calls=%async_computation.2 | async-start | bytes 10485760 | tf_op jit(solution)/shard_map/slice | solution.py:510
  15.8 8.8 %collective-permute-start.6 = (bf16[2,8,3072]{2,1,0:T(8,128)(2,1)S(1)}, bf16[2,8,3072]{2,1,0:T(8,128)(2,1)S(1)}, u32[]{:S(2)}, u32[]{:S(2)}) collective-permute-start(bf16[2,8,3072]{2,1,0:T(8,128)(2,1)S(1)} %pad_maximum_fusion.2), channel_id=1, source_target_pairs={{0,8},{1,9},{2,10},{3,11},{4,12},{5,13},{6,14},{7,15},{8,0},{9,1},... | collective-permute-start | bytes 294920 | tf_op jit(solution)/shard_map/ppermute | solution.py:481
  17.3 7.3 %collective-permute-start.7 = (bf16[2,8,3072]{2,1,0:T(8,128)(2,1)S(1)}, bf16[2,8,3072]{2,1,0:T(8,128)(2,1)S(1)}, u32[]{:S(2)}, u32[]{:S(2)}) collective-permute-start(bf16[2,8,3072]{2,1,0:T(8,128)(2,1)S(1)} %pad_maximum_fusion.2), channel_id=1, source_target_pairs={{0,12},{1,13},{2,14},{3,15},{4,0},{5,1},{6,2},{7,3},{8,4},{9,5},{1... | collective-permute-start | bytes 294920 | tf_op jit(solution)/shard_map/ppermute | solution.py:481
  19.1 1.9 %slice-start.3 = ((bf16[8192,4,128]{2,1,0:T(4,128)(2,1)}), bf16[3072,4,128]{2,1,0:T(4,128)(2,1)S(1)}, s32[]{:S(2)}) async-start(bf16[8192,4,128]{2,1,0:T(4,128)(2,1)} %param.13), calls=%async_computation.3 | async-start | bytes 6291456 | tf_op jit(solution)/shard_map/slice | solution.py:511
  21.5 8.2 %collective-permute-start.4 = (bf16[32,5120]{1,0:T(8,128)(2,1)S(1)}, bf16[32,5120]{1,0:T(8,128)(2,1)S(1)}, u32[]{:S(2)}, u32[]{:S(2)}) collective-permute-start(bf16[32,5120]{1,0:T(8,128)(2,1)S(1)} %bitcast.71), channel_id=1, source_target_pairs={{0,2},{1,3},{2,0},{3,1},{4,6},{5,7},{6,4},{7,5},{8,10},{9,11},{10,... | collective-permute-start | bytes 983048 | tf_op jit(solution)/shard_map/ppermute | solution.py:481
  29.7 2.7 %collective-permute-start.10 = (bf16[64,3072]{1,0:T(8,128)(2,1)S(1)}, bf16[64,3072]{1,0:T(8,128)(2,1)S(1)}, u32[]{:S(2)}, u32[]{:S(2)}) collective-permute-start(bf16[64,3072]{1,0:T(8,128)(2,1)S(1)} %bitcast.68), channel_id=1, source_target_pairs={{0,1},{1,0},{2,3},{3,2},{4,5},{5,4},{6,7},{7,6},{8,9},{9,8},{10,11... | collective-permute-start | bytes 1179656 | tf_op jit(solution)/shard_map/ppermute | solution.py:481
  29.7 2.2 %collective-permute-start.8 = (bf16[32,5120]{1,0:T(8,128)(2,1)S(1)}, bf16[32,5120]{1,0:T(8,128)(2,1)S(1)}, u32[]{:S(2)}, u32[]{:S(2)}) collective-permute-start(bf16[32,5120]{1,0:T(8,128)(2,1)S(1)} %bitcast.72), channel_id=1, source_target_pairs={{0,1},{1,0},{2,3},{3,2},{4,5},{5,4},{6,7},{7,6},{8,9},{9,8},{10,11... | collective-permute-start | bytes 983048 | tf_op jit(solution)/shard_map/ppermute | solution.py:481
  30.2 2.1 %collective-permute-start.9 = (bf16[32,5120]{1,0:T(8,128)(2,1)S(1)}, bf16[32,5120]{1,0:T(8,128)(2,1)S(1)}, u32[]{:S(2)}, u32[]{:S(2)}) collective-permute-start(bf16[32,5120]{1,0:T(8,128)(2,1)S(1)} %collective-permute-done.4.a1), channel_id=1, source_target_pairs={{0,1},{1,0},{2,3},{3,2},{4,5},{5,4},{6,7},{7,6},{8,9},{9,8},{10,11... | collective-permute-start | bytes 983048 | tf_op jit(solution)/shard_map/ppermute | solution.py:481
  32.9 2.0 %collective-permute-start.11 = (bf16[128,1024]{1,0:T(8,128)(2,1)S(1)}, bf16[128,1024]{1,0:T(8,128)(2,1)S(1)}, u32[]{:S(2)}, u32[]{:S(2)}) collective-permute-start(bf16[128,1024]{1,0:T(8,128)(2,1)S(1)} %get-tuple-element.39), channel_id=1, source_target_pairs={{0,1},{1,0},{2,3},{3,2},{4,5},{5,4},{6,7},{7,6},{8,9},{9,8},{10,11... | collective-permute-start | bytes 786440 | tf_op jit(solution)/shard_map/ppermute | solution.py:481
  34.8 19.3 %copy-start = (bf16[1,6,2048,128]{3,2,1,0:T(8,128)(2,1)S(1)}, bf16[1,6,2048,128]{3,2,1,0:T(8,128)(2,1)}, u32[]{:S(2)}) copy-start(bf16[1,6,2048,128]{3,2,1,0:T(8,128)(2,1)} %refs_5_.1) | copy-start | bytes 9437188
  34.8 19.3 %copy-start.1 = (bf16[1,6,2048,128]{3,2,1,0:T(8,128)(2,1)S(1)}, bf16[1,6,2048,128]{3,2,1,0:T(8,128)(2,1)}, u32[]{:S(2)}) copy-start(bf16[1,6,2048,128]{3,2,1,0:T(8,128)(2,1)} %refs_6_.1) | copy-start | bytes 9437188
  34.8 19.3 %copy-start.5 = (s32[12]{0:T(128)S(1)}, s32[12]{0:T(128)}, u32[]{:S(2)}) copy-start(s32[12]{0:T(128)} %counts_ref.1) | copy-start | bytes 148
  34.8 19.3 %copy-start.6 = (s32[128]{0:T(128)S(1)}, s32[128]{0:T(128)}, u32[]{:S(2)}) copy-start(s32[128]{0:T(128)} %lens_ref.1) | copy-start | bytes 1540
  35.0 5.9 %collective-permute-start.12 = (bf16[128,512]{1,0:T(8,128)(2,1)S(1)}, bf16[128,512]{1,0:T(8,128)(2,1)S(1)}, u32[]{:S(2)}, u32[]{:S(2)}) collective-permute-start(bf16[128,512]{1,0:T(8,128)(2,1)S(1)} %pad_maximum_fusion.1), channel_id=1, source_target_pairs={{0,2},{1,3},{2,0},{3,1},{4,6},{5,7},{6,4},{7,5},{8,10},{9,11},{10,... | collective-permute-start | bytes 393224 | tf_op jit(solution)/shard_map/ppermute | solution.py:481
  40.9 4.3 %collective-permute-start.15 = (bf16[128,256]{1,0:T(8,128)(2,1)S(1)}, bf16[128,256]{1,0:T(8,128)(2,1)S(1)}, u32[]{:S(2)}, u32[]{:S(2)}) collective-permute-start(bf16[128,256]{1,0:T(8,128)(2,1)S(1)} %slice.159), channel_id=1, source_target_pairs={{0,4},{1,5},{2,6},{3,7},{4,0},{5,1},{6,2},{7,3},{8,12},{9,13},{10,... | collective-permute-start | bytes 196616 | tf_op jit(solution)/shard_map/ppermute | solution.py:481
  45.2 6.4 %collective-permute-start.16 = (bf16[128,256]{1,0:T(8,128)(2,1)S(1)}, bf16[128,256]{1,0:T(8,128)(2,1)S(1)}, u32[]{:S(2)}, u32[]{:S(2)}) collective-permute-start(bf16[128,256]{1,0:T(8,128)(2,1)S(1)} %fusion.4), channel_id=1, source_target_pairs={{0,8},{1,9},{2,10},{3,11},{4,12},{5,13},{6,14},{7,15},{8,0},{9,1},... | collective-permute-start | bytes 196616 | tf_op jit(solution)/shard_map/ppermute | solution.py:481
  46.7 5.0 %collective-permute-start.13 = (bf16[128,512]{1,0:T(8,128)(2,1)S(1)}, bf16[128,512]{1,0:T(8,128)(2,1)S(1)}, u32[]{:S(2)}, u32[]{:S(2)}) collective-permute-start(bf16[128,512]{1,0:T(8,128)(2,1)S(1)} %shard_map.112), channel_id=1, source_target_pairs={{0,0},{1,8},{2,1},{3,9},{4,2},{5,10},{6,3},{7,11},{8,4},{9,12},{10... | collective-permute-start | bytes 393224 | tf_op jit(solution)/shard_map/ppermute | solution.py:481
  47.3 6.8 %collective-permute-start.14 = (bf16[128,512]{1,0:T(8,128)(2,1)S(1)}, bf16[128,512]{1,0:T(8,128)(2,1)S(1)}, u32[]{:S(2)}, u32[]{:S(2)}) collective-permute-start(bf16[128,512]{1,0:T(8,128)(2,1)S(1)} %shard_map.112), channel_id=1, source_target_pairs={{0,8},{1,0},{2,9},{3,1},{4,10},{5,2},{6,11},{7,3},{8,12},{9,4},{10... | collective-permute-start | bytes 393224 | tf_op jit(solution)/shard_map/ppermute | solution.py:481
  51.6 25.0 %slice-start = ((s8[8388608]{0:T(1024)(128)(4,1)}), s8[4194304]{0:T(1024)(128)(4,1)S(1)}, s32[]{:S(2)}) async-start(s8[8388608]{0:T(1024)(128)(4,1)} %bitcast.65), calls=%async_computation | async-start | bytes 8388608
  51.6 25.0 %slice-start.1 = ((s8[8388608]{0:T(1024)(128)(4,1)}), s8[4194304]{0:T(1024)(128)(4,1)S(1)}, s32[]{:S(2)}) async-start(s8[8388608]{0:T(1024)(128)(4,1)} %bitcast.65), calls=%async_computation.1 | async-start | bytes 8388608
  66.0 4.7 %collective-permute-start.17 = (bf16[128,512]{1,0:T(8,128)(2,1)S(1)}, bf16[128,512]{1,0:T(8,128)(2,1)S(1)}, u32[]{:S(2)}, u32[]{:S(2)}) collective-permute-start(bf16[128,512]{1,0:T(8,128)(2,1)S(1)} %get-tuple-element.49), channel_id=1, source_target_pairs={{0,0},{8,1},{1,2},{9,3},{2,4},{10,5},{3,6},{11,7},{4,8},{12,9},{5,... | collective-permute-start | bytes 393224 | tf_op jit(solution)/shard_map/ppermute | solution.py:481
  66.7 9.9 %collective-permute-start.18 = (bf16[128,512]{1,0:T(8,128)(2,1)S(1)}, bf16[128,512]{1,0:T(8,128)(2,1)S(1)}, u32[]{:S(2)}, u32[]{:S(2)}) collective-permute-start(bf16[128,512]{1,0:T(8,128)(2,1)S(1)} %get-tuple-element.50), channel_id=1, source_target_pairs={{8,0},{0,1},{9,2},{1,3},{10,4},{2,5},{11,6},{3,7},{12,8},{4,9},{13... | collective-permute-start | bytes 393224 | tf_op jit(solution)/shard_map/ppermute | solution.py:481
  80.1 29.1 %copy-start.3 = (bf16[8,8192]{1,0:T(8,128)(2,1)S(1)}, bf16[8,8192]{1,0:T(8,128)(2,1)}, u32[]{:S(2)}) copy-start(bf16[8,8192]{1,0:T(8,128)(2,1)} %x_ref.1) | copy-start | bytes 393220
  80.1 2.7 %collective-permute-start.19 = (bf16[64,8192]{1,0:T(8,128)(2,1)S(1)}, bf16[64,8192]{1,0:T(8,128)(2,1)S(1)}, u32[]{:S(2)}, u32[]{:S(2)}) collective-permute-start(bf16[64,8192]{1,0:T(8,128)(2,1)S(1)} %get-tuple-element.52), channel_id=1, source_target_pairs={{0,1},{1,0},{2,3},{3,2},{4,5},{5,4},{6,7},{7,6},{8,9},{9,8},{10,11... | collective-permute-start | bytes 3145736 | tf_op jit(solution)/shard_map/ppermute | solution.py:481
  83.0 9.1 %collective-permute-start.24 = (bf16[2,8,3072]{2,1,0:T(8,128)(2,1)S(1)}, bf16[2,8,3072]{2,1,0:T(8,128)(2,1)S(1)}, u32[]{:S(2)}, u32[]{:S(2)}) collective-permute-start(bf16[2,8,3072]{2,1,0:T(8,128)(2,1)S(1)} %get-tuple-element.59), channel_id=1, source_target_pairs={{0,4},{1,5},{2,6},{3,7},{4,8},{5,9},{6,10},{7,11},{8,12},{9,13},{1... | collective-permute-start | bytes 294920 | tf_op jit(solution)/shard_map/ppermute | solution.py:481
  88.2 7.7 %collective-permute-start.25 = (bf16[2,8,3072]{2,1,0:T(8,128)(2,1)S(1)}, bf16[2,8,3072]{2,1,0:T(8,128)(2,1)S(1)}, u32[]{:S(2)}, u32[]{:S(2)}) collective-permute-start(bf16[2,8,3072]{2,1,0:T(8,128)(2,1)S(1)} %get-tuple-element.60), channel_id=1, source_target_pairs={{0,8},{1,9},{2,10},{3,11},{4,12},{5,13},{6,14},{7,15},{8,0},{9,1},... | collective-permute-start | bytes 294920 | tf_op jit(solution)/shard_map/ppermute | solution.py:481
  88.2 7.7 %collective-permute-start.26 = (bf16[2,8,3072]{2,1,0:T(8,128)(2,1)S(1)}, bf16[2,8,3072]{2,1,0:T(8,128)(2,1)S(1)}, u32[]{:S(2)}, u32[]{:S(2)}) collective-permute-start(bf16[2,8,3072]{2,1,0:T(8,128)(2,1)S(1)} %get-tuple-element.61), channel_id=1, source_target_pairs={{0,12},{1,13},{2,14},{3,15},{4,0},{5,1},{6,2},{7,3},{8,4},{9,5},{1... | collective-permute-start | bytes 294920 | tf_op jit(solution)/shard_map/ppermute | solution.py:481
  90.7 10.0 %collective-permute-start.20 = (bf16[32,5120]{1,0:T(8,128)(2,1)S(1)}, bf16[32,5120]{1,0:T(8,128)(2,1)S(1)}, u32[]{:S(2)}, u32[]{:S(2)}) collective-permute-start(bf16[32,5120]{1,0:T(8,128)(2,1)S(1)} %add_convert_fusion.1), channel_id=1, source_target_pairs={{0,2},{1,3},{2,0},{3,1},{4,6},{5,7},{6,4},{7,5},{8,10},{9,11},{10,... | collective-permute-start | bytes 983048 | tf_op jit(solution)/shard_map/ppermute | solution.py:481
  95.9 8.8 %collective-permute-start.27 = (bf16[8,3072]{1,0:T(8,128)(2,1)S(1)}, bf16[8,3072]{1,0:T(8,128)(2,1)S(1)}, u32[]{:S(2)}, u32[]{:S(2)}) collective-permute-start(bf16[8,3072]{1,0:T(8,128)(2,1)S(1)} %fusion.5), channel_id=1, source_target_pairs={{0,2},{1,3},{2,0},{3,1},{4,6},{5,7},{6,4},{7,5},{8,10},{9,11},{10,... | collective-permute-start | bytes 147464 | tf_op jit(solution)/shard_map/ppermute | solution.py:481
  100.9 6.5 %collective-permute-start.21 = (bf16[8,5120]{1,0:T(8,128)(2,1)S(1)}, bf16[8,5120]{1,0:T(8,128)(2,1)S(1)}, u32[]{:S(2)}, u32[]{:S(2)}) collective-permute-start(bf16[8,5120]{1,0:T(8,128)(2,1)S(1)} %get-tuple-element.62), channel_id=1, source_target_pairs={{0,4},{1,5},{2,6},{3,7},{4,8},{5,9},{6,10},{7,11},{8,12},{9,13},{1... | collective-permute-start | bytes 245768 | tf_op jit(solution)/shard_map/ppermute | solution.py:481
  100.9 8.1 %collective-permute-start.22 = (bf16[8,5120]{1,0:T(8,128)(2,1)S(1)}, bf16[8,5120]{1,0:T(8,128)(2,1)S(1)}, u32[]{:S(2)}, u32[]{:S(2)}) collective-permute-start(bf16[8,5120]{1,0:T(8,128)(2,1)S(1)} %get-tuple-element.64), channel_id=1, source_target_pairs={{0,8},{1,9},{2,10},{3,11},{4,12},{5,13},{6,14},{7,15},{8,0},{9,1},... | collective-permute-start | bytes 245768 | tf_op jit(solution)/shard_map/ppermute | solution.py:481
  102.6 6.4 %collective-permute-start.23 = (bf16[8,5120]{1,0:T(8,128)(2,1)S(1)}, bf16[8,5120]{1,0:T(8,128)(2,1)S(1)}, u32[]{:S(2)}, u32[]{:S(2)}) collective-permute-start(bf16[8,5120]{1,0:T(8,128)(2,1)S(1)} %get-tuple-element.63), channel_id=1, source_target_pairs={{0,12},{1,13},{2,14},{3,15},{4,0},{5,1},{6,2},{7,3},{8,4},{9,5},{1... | collective-permute-start | bytes 245768 | tf_op jit(solution)/shard_map/ppermute | solution.py:481
where the time goes:
time: 110 us
  starting transfers between devices  41.9 us (38%)
  waiting for transfers between devices  38.6 us (35%)
  Pallas kernels  18.8 us (17%)
  local copies, waits for them, and re-layouts  7.64 us (7%)
  other arithmetic  2.36 us (2%)
    ppermute x28, starting transfers between devices, move(): return lax.ppermute(x, 'tensor', pairs)  41.9 us
    ppermute x28, waiting for transfers between devices, move(): return lax.ppermute(x, 'tensor', pairs)  38.6 us
    pallas_call x1, Pallas kernels, attend(): pl.pallas_call(functools.partial(attend_kernel, groups, kvh, hs), out_sha...  11.9 us
    pallas_call x1, Pallas kernels, output_product(): pl.pallas_call(functools.partial(output_kernel, groups, zn), grid=(cols /...  3.41 us
    reshape x1, local copies, waits for them, and re-layouts, local(): wkv = w_kv.reshape(slab, kvh * 2 * hd)  3.3 us
    unnamed x20, local copies, waits for them, and re-layouts  3.11 us
  transfers between devices with their start and end apart: 28, of which 14 were waited for; matrix products, arithmetic and copies ran while one was open for 6% of the time, Pallas kernels for 3%

commit v1 on v0

--- a/solution.py
+++ b/solution.py
@@ -205,6 +205,14 @@
     )(*far, wq, half)
 
 
+def rope(x, cosines, sines):
+    return x * cosines + pltpu.roll(x, x.shape[1] // 2, 1) * sines
+
+
+def rounded(x):
+    return x.astype(BF16).astype(F32)
+
+
 def trips(work, cap):
     for b in range(cap // CHUNK):
         work(b, 0)
@@ -214,9 +222,8 @@
     groups, kvh, hs, counts_ref, lens_ref, *refs
 ):
     q_in = refs[:groups]
-    kv_ref, cos_ref, sin_ref, pk_ref, pv_ref, sk_ref, sv_ref = refs[groups : groups + 7]
-    outs = refs[groups + 7 : 2 * groups + 7]
-    q_sc, k_sc, v_sc, o_sc, ss_sc, sp_sc, ac_sc, key_buf, value_buf, sems = refs[2 * groups + 7 :]
+    cos_ref, sin_ref, pk_ref, pv_ref, sk_ref, sv_ref = refs[groups : groups + 6]
+    q_sc, o_sc, stat_sc, ss_sc, sp_sc, ac_sc, key_buf, value_buf, sems = refs[groups + 6 :]
     step = pl.program_id(0)
     me = lax.axis_index("tensor")
     group = lax.div(me, kvh)
@@ -226,12 +233,6 @@
     smax = sk_ref.shape[2]
     scaling = 1.0 / math.sqrt(hd)
 
-    def rope(x, cosines, sines):
-        return x * cosines + pltpu.roll(x, hd // 2, 1) * sines
-
-    def rounded(x):
-        return x.astype(BF16).astype(F32)
-
     def fetch(p, c, kind):
         source, target = ((sk_ref, key_buf), (sv_ref, value_buf))[kind]
         span = pl.ds(p * PCAP + c * CHUNK, CHUNK)
@@ -252,9 +253,8 @@
 
         cosines, sines = cos_ref[...], sin_ref[...]
         q_sc[pl.ds(rows, PCAP + 3)] = jnp.zeros((PCAP + 3, heads, hd), F32)
-        k_sc[pl.ds(rows, PCAP + 3)] = jnp.zeros((PCAP + 3, heads, hd), F32)
-        v_sc[pl.ds(rows, PCAP + 3)] = jnp.zeros((PCAP + 3, heads, hd), F32)
         o_sc[...] = jnp.zeros_like(o_sc)
+        stat_sc[...] = jnp.zeros_like(stat_sc)
         for s in range(groups):
             which = lax.rem(group - s + groups, groups)
             for j in range(hs):
@@ -263,11 +263,6 @@
                 for k in range(1, groups):
                     x = jnp.where(which == k, q_in[k][:, cols], x)
                 q_sc[pl.ds(0, rows), s * hs + j] = rounded(rope(x.astype(F32), cosines, sines))
-        key = rounded(rope(rounded(kv_ref[:, :hd]), cosines, sines))
-        value = rounded(kv_ref[:, hd:])
-        for j in range(heads):
-            k_sc[pl.ds(0, rows), j] = key
-            v_sc[pl.ds(0, rows), j] = value
 
     prompt = group * PROM_DEV + step
     start = lax.fori_loop(0, prompt, lambda p, t: t + counts_ref[p], 0)
@@ -279,8 +274,6 @@
     def prompt_rows(cap):
         flat = cap * heads
         q_wide = q_sc[pl.ds(start, cap)].reshape(flat, hd)
-        k_wide = k_sc[pl.ds(start, cap)].reshape(flat, hd)
-        own = jnp.sum(q_wide * k_wide, axis=1, keepdims=True) * scaling
         scores = (
             lax.dot_general(
                 q_wide.astype(BF16), pk_ref[0, 0], contract, preferred_element_type=F32
@@ -305,21 +298,14 @@
         trips(score_rows, cap)
         tail = ss_sc[:cap].reshape(flat, smax)
         highest = jnp.maximum(
-            jnp.max(scores, axis=1, keepdims=True),
-            jnp.maximum(jnp.max(tail, axis=1, keepdims=True), own),
+            jnp.max(scores, axis=1, keepdims=True), jnp.max(tail, axis=1, keepdims=True)
         )
         past_exp = jnp.exp(scores - highest)
         tail_exp = jnp.exp(tail - highest)
-        own_exp = jnp.exp(own - highest)
-        total = (
-            jnp.sum(past_exp, axis=1, keepdims=True)
-            + jnp.sum(tail_exp, axis=1, keepdims=True)
-            + own_exp
-        )
+        total = jnp.sum(past_exp, axis=1, keepdims=True) + jnp.sum(tail_exp, axis=1, keepdims=True)
         inverse = 1.0 / total
         sp_sc[:cap] = (tail_exp * inverse).reshape(cap, heads, smax)
         past_weights = (past_exp * inverse).astype(BF16)
-        own_weight = rounded(own_exp * inverse)
         result = jnp.dot(past_weights, pv_ref[0, 0], preferred_element_type=F32)
 
         def mix_rows(b, carry):
@@ -333,13 +319,12 @@
         for c in range(cap // CHUNK):
             fetch(step, c, 1).wait()
         trips(mix_rows, cap)
-        result = (
-            result
-            + ac_sc[:cap].reshape(flat, hd)
-            + own_weight * v_sc[pl.ds(start, cap)].reshape(flat, hd)
-        )
+        result = result + ac_sc[:cap].reshape(flat, hd)
+        lane = lax.broadcasted_iota(jnp.int32, (flat, hd), 1)
+        stat = jnp.where(lane < hd // 2, highest, total)
         slot = lax.broadcasted_iota(jnp.int32, (cap, heads, hd), 0)
         o_sc[pl.ds(start, cap)] = jnp.where(slot < count, result.reshape(cap, heads, hd), 0.0)
+        stat_sc[pl.ds(start, cap)] = jnp.where(slot < count, stat.reshape(cap, heads, hd), 0.0)
 
     for c in range(CHUNKS):
 
@@ -347,18 +332,51 @@
         def _(c=c):
             prompt_rows((c + 1) * CHUNK)
 
-    @pl.when(step == pl.num_programs(0) - 1)
-    def _():
-        for k in range(groups):
-            which = lax.rem(group - k + groups, groups)
-            for j in range(hs):
-                x = o_sc[pl.ds(0, rows), j]
-                for s in range(1, groups):
-                    x = jnp.where(which == s, o_sc[pl.ds(0, rows), s * hs + j], x)
-                outs[k][:, j * hd : (j + 1) * hd] = x.astype(BF16)
-
-
-def attend(groups, kvh, counts, lengths, queries, kv, cosines, sines, pk, pv, sk, sv):
+
+def merge_kernel(groups, kvh, kv_ref, cos_ref, sin_ref, q_ref, o_ref, stat_ref, *outs):
+    group = lax.div(lax.axis_index("tensor"), kvh)
+    rows, hd = cos_ref.shape
+    heads = q_ref.shape[1]
+    hs = heads // groups
+    key = rounded(rope(rounded(kv_ref[:, :hd]), cos_ref[...], sin_ref[...]))
+    value = rounded(kv_ref[:, hd:])
+    found = pl.ds(0, rows)
+    merged = []
+    for j in range(heads):
+        own = jnp.sum(q_ref[found, j] * key, axis=1, keepdims=True) * (1.0 / math.sqrt(hd))
+        stat = stat_ref[found, j]
+        past, total = stat[:, :1], stat[:, hd // 2 : hd // 2 + 1]
+        highest = jnp.maximum(past, own)
+        past_exp = jnp.exp(past - highest) * total
+        own_exp = jnp.exp(own - highest)
+        inverse = 1.0 / (past_exp + own_exp)
+        result = o_ref[found, j] * (past_exp * inverse) + rounded(own_exp * inverse) * value
+        merged.append(jnp.where(total > 0, result, 0.0))
+    for k in range(groups):
+        which = lax.rem(group - k + groups, groups)
+        for j in range(hs):
+            x = merged[j]
+            for s in range(1, groups):
+                x = jnp.where(which == s, merged[s * hs + j], x)
+            outs[k][:, j * hd : (j + 1) * hd] = x.astype(BF16)
+
+
+def merge(groups, kvh, kv, cosines, sines, queries, mixed, stats):
+    rows, hd = cosines.shape
+    share = queries.shape[1] // groups * hd
+    return pl.pallas_call(
+        functools.partial(merge_kernel, groups, kvh),
+        out_shape=tuple(jax.ShapeDtypeStruct((rows, share), BF16) for _ in range(groups)),
+        in_specs=[vmem()] * 6,
+        out_specs=(vmem(),) * groups,
+        compiler_params=room(16),
+        cost_estimate=pl.CostEstimate(
+            flops=20 * queries.size, bytes_accessed=16 * queries.size, transcendentals=0
+        ),
+    )(kv, cosines, sines, queries, mixed, stats)
+
+
+def attend(groups, kvh, counts, lengths, queries, cosines, sines, pk, pv, sk, sv):
     rows, share = queries[0].shape
     hd = cosines.shape[1]
     hs = share // hd
@@ -369,17 +387,16 @@
     piece = lambda a, n: pl.BlockSpec((1, n) + a.shape[2:], lambda i, *_: (0, i, 0, 0))
     return pl.pallas_call(
         functools.partial(attend_kernel, groups, kvh, hs),
-        out_shape=tuple(jax.ShapeDtypeStruct((rows, share), BF16) for _ in range(groups)),
+        out_shape=(jax.ShapeDtypeStruct((pads, heads, hd), F32),) * 3,
         grid_spec=pltpu.PrefetchScalarGridSpec(
             num_scalar_prefetch=2,
             grid=(PROM_DEV,),
             in_specs=[const(q.shape) for q in queries]
-            + [const(kv.shape), const(cosines.shape), const(sines.shape)]
+            + [const(cosines.shape), const(sines.shape)]
             + [piece(pk, 1), piece(pv, 1)]
             + [pl.BlockSpec(memory_space=pltpu.HBM)] * 2,
-            out_specs=tuple(const((rows, share)) for _ in range(groups)),
-            scratch_shapes=[pltpu.VMEM((pads, heads, hd), F32)] * 4
-            + [
+            out_specs=(const((pads, heads, hd)),) * 3,
+            scratch_shapes=[
                 pltpu.VMEM((PCAP, heads, smax), F32),
                 pltpu.VMEM((PCAP, heads, smax), F32),
                 pltpu.VMEM((PCAP, heads, hd), F32),
@@ -394,7 +411,7 @@
             bytes_accessed=2 * (pk.size + pv.size + sk.size + sv.size),
             transcendentals=PROM_DEV * PCAP * heads * (PREFIX + smax),
         ),
-    )(counts, lengths, *queries, kv, cosines, sines, pk, pv, sk, sv)
+    )(counts, lengths, *queries, cosines, sines, pk, pv, sk, sv)
 
 
 def output_kernel(groups, zn, *refs):
@@ -540,28 +557,27 @@
     total = keep + came.astype(F32)
     came = swap(blocks(total, 1).astype(BF16), CORES)
     query = query_far(far_pieces, wq_far, half)
-    came, query = lax.optimization_barrier((came, query))
+    came, _ = lax.optimization_barrier((came, query))
     total = blocks(total, 0) + came.astype(F32)
     received = [
         move(query, [(i, ((i % groups + k) % groups) * kvh + i // groups) for i in range(devices)])
         for k in range(groups)
     ]
     bit = CORES
+    while bit * 2 < kvh:
+        bit *= 2
+        total = blocks(total, 0) + swap(blocks(total, 1).astype(BF16), bit).astype(F32)
+    total, received[0] = lax.optimization_barrier((total, received[0]))
+    fresh = total
     while bit * 2 < devices:
         bit *= 2
-        if bit < kvh:
-            total = blocks(total, 0) + swap(blocks(total, 1).astype(BF16), bit).astype(F32)
-        else:
-            sent = total.astype(BF16)
-            total = total + swap(sent, bit).astype(F32)
-
-    attended = attend(
+        fresh = fresh + swap(fresh.astype(BF16), bit).astype(F32)
+    queries, mixed, stats = attend(
         groups,
         kvh,
         row_counts,
         suffix_lengths,
         received,
-        total,
         cosines,
         sines,
         prefix_keys,
@@ -569,6 +585,7 @@
         suffix_keys,
         suffix_values,
     )
+    attended = merge(groups, kvh, fresh, cosines, sines, queries, mixed, stats)
     parts = [
         move(
             attended[k],

time: 110 us -> 108 us (0.982)
  waiting for transfers between devices: 38.6 us -> 31.2 us
  starting transfers between devices: 41.9 us -> 45.3 us
  Pallas kernels: 18.8 us -> 20.9 us
    ppermute x28, waiting for transfers between devices: 38.6 us -> 31.2 us  [move(): return lax.ppermute(x, 'tensor', pairs)]
    ppermute x28, starting transfers between devices: 41.9 us -> 45.3 us  [move(): return lax.ppermute(x, 'tensor', pairs)]
    pallas_call x0 -> x1, Pallas kernels: none -> 3.15 us  [merge(): pl.pallas_call(functools.partial(merge_kernel, groups, kvh), out_shape=tu...]
  transfers between devices with their start and end apart: 28 -> 28, of which waited for: 14 -> 13; matrix products, arithmetic and copies ran while one was open for 6% -> 6% of each run, Pallas kernels for 3% -> 13%
where the time goes in v1:
time: 108 us
  starting transfers between devices  45.3 us (42%)
  waiting for transfers between devices  31.2 us (29%)
  Pallas kernels  20.9 us (19%)
  local copies, waits for them, and re-layouts  7.64 us (7%)
  other arithmetic  2.37 us (2%)
    ppermute x28, starting transfers between devices, move(): return lax.ppermute(x, 'tensor', pairs)  45.3 us
    ppermute x28, waiting for transfers between devices, move(): return lax.ppermute(x, 'tensor', pairs)  31.2 us
    pallas_call x1, Pallas kernels, attend(): pl.pallas_call(functools.partial(attend_kernel, groups, kvh, hs), out_sha...  10.8 us
    pallas_call x1, Pallas kernels, output_product(): pl.pallas_call(functools.partial(output_kernel, groups, zn), grid=(cols /...  3.42 us
    reshape x1, local copies, waits for them, and re-layouts, local(): wkv = w_kv.reshape(slab, kvh * 2 * hd)  3.3 us
    pallas_call x1, Pallas kernels, merge(): pl.pallas_call(functools.partial(merge_kernel, groups, kvh), out_shape=tu...  3.15 us
    unnamed x20, local copies, waits for them, and re-layouts  3.11 us
  transfers between devices with their start and end apart: 28, of which 13 were waited for; matrix products, arithmetic and copies ran while one was open for 6% of the time, Pallas kernels for 13%

profile of v1, /device:TPU:0, one launch (start us, length us, event | category | flops | bytes accessed | tf_op | source)
XLA Modules:
  0.0 107.9 jit_solution(4716029346405626948)
XLA Ops:
  0.0 0.9 copy-done.2
  0.9 0.7 copy-done.4
  1.6 0.2 shard_map.109
  1.8 3.1 %collective-permute-start = (bf16[8,5120]{1,0:T(8,128)(2,1)S(1)}, bf16[8,5120]{1,0:T(8,128)(2,1)S(1)}, u32[]{:S(2)}, u32[]{:S(2)}) collective-permute-start(bf16[8,5120]{1,0:T(8,128)(2,1)S(1)} %get-tuple-element.33), channel_id=1, source_target_pairs={{0,4},{1,5},{2,6},{3,7},{4,8},{5,9},{6,10},{7,11},{8,12},{9,13},{1... | collective-permute-start | bytes 245768 | tf_op jit(solution)/shard_map/ppermute | solution.py:498
  4.9 2.6 %collective-permute-start.1 = (bf16[8,5120]{1,0:T(8,128)(2,1)S(1)}, bf16[8,5120]{1,0:T(8,128)(2,1)S(1)}, u32[]{:S(2)}, u32[]{:S(2)}) collective-permute-start(bf16[8,5120]{1,0:T(8,128)(2,1)S(1)} %get-tuple-element.33), channel_id=1, source_target_pairs={{0,8},{1,9},{2,10},{3,11},{4,12},{5,13},{6,14},{7,15},{8,0},{9,1},... | collective-permute-start | bytes 245768 | tf_op jit(solution)/shard_map/ppermute | solution.py:498
  7.5 1.3 %collective-permute-start.2 = (bf16[8,5120]{1,0:T(8,128)(2,1)S(1)}, bf16[8,5120]{1,0:T(8,128)(2,1)S(1)}, u32[]{:S(2)}, u32[]{:S(2)}) collective-permute-start(bf16[8,5120]{1,0:T(8,128)(2,1)S(1)} %get-tuple-element.33), channel_id=1, source_target_pairs={{0,12},{1,13},{2,14},{3,15},{4,0},{5,1},{6,2},{7,3},{8,4},{9,5},{1... | collective-permute-start | bytes 245768 | tf_op jit(solution)/shard_map/ppermute | solution.py:498
  8.9 1.5 %collective-permute-start.3 = (bf16[8,3072]{1,0:T(8,128)(2,1)S(1)}, bf16[8,3072]{1,0:T(8,128)(2,1)S(1)}, u32[]{:S(2)}, u32[]{:S(2)}) collective-permute-start(bf16[8,3072]{1,0:T(8,128)(2,1)S(1)} %get-tuple-element.34), channel_id=1, source_target_pairs={{0,2},{1,3},{2,0},{3,1},{4,6},{5,7},{6,4},{7,5},{8,10},{9,11},{10,... | collective-permute-start | bytes 147464 | tf_op jit(solution)/shard_map/ppermute | solution.py:498
  10.4 0.7 add_convert_fusion.5
  11.1 0.3 fusion.5
  11.4 0.1 pad_maximum_fusion.3
  11.6 3.3 %reshape.41.wkv_ref = bf16[512,2048]{1,0:T(8,128)(2,1)S(1)} reshape(bf16[512,8,2,128]{3,2,1,0:T(2,128)(2,1)} %param.14) | data formatting | bytes 4194304 | tf_op jit(solution)/shard_map/reshape | solution.py:506
  15.0 0.7 collective-permute-start.5
  15.8 0.0 slice-start.2
  15.8 1.5 %collective-permute-start.6 = (bf16[2,8,3072]{2,1,0:T(8,128)(2,1)S(1)}, bf16[2,8,3072]{2,1,0:T(8,128)(2,1)S(1)}, u32[]{:S(2)}, u32[]{:S(2)}) collective-permute-start(bf16[2,8,3072]{2,1,0:T(8,128)(2,1)S(1)} %pad_maximum_fusion.2), channel_id=1, source_target_pairs={{0,8},{1,9},{2,10},{3,11},{4,12},{5,13},{6,14},{7,15},{8,0},{9,1},... | collective-permute-start | bytes 294920 | tf_op jit(solution)/shard_map/ppermute | solution.py:498
  17.3 1.8 %collective-permute-start.7 = (bf16[2,8,3072]{2,1,0:T(8,128)(2,1)S(1)}, bf16[2,8,3072]{2,1,0:T(8,128)(2,1)S(1)}, u32[]{:S(2)}, u32[]{:S(2)}) collective-permute-start(bf16[2,8,3072]{2,1,0:T(8,128)(2,1)S(1)} %pad_maximum_fusion.2), channel_id=1, source_target_pairs={{0,12},{1,13},{2,14},{3,15},{4,0},{5,1},{6,2},{7,3},{8,4},{9,5},{1... | collective-permute-start | bytes 294920 | tf_op jit(solution)/shard_map/ppermute | solution.py:498
  19.1 0.9 copy.28
  20.0 1.0 slice-done.3
  21.0 0.5 copy.29
  21.5 0.6 collective-permute-start.4
  22.1 0.4 collective-permute-done.5
  22.5 2.1 %collective-permute-done.6 = bf16[2,8,3072]{2,1,0:T(8,128)(2,1)S(1)} collective-permute-done((bf16[2,8,3072]{2,1,0:T(8,128)(2,1)S(1)}, bf16[2,8,3072]{2,1,0:T(8,128)(2,1)S(1)}, u32[]{:S(2)}, u32[]{:S(2)}) %collective-permute-start.6) | collective-permute-done | bytes 98336 | tf_op jit(solution)/shard_map/ppermute | solution.py:498
  24.6 5.1 %collective-permute-done.4.a1 = bf16[32,5120]{1,0:T(8,128)(2,1)S(1)} collective-permute-done((bf16[32,5120]{1,0:T(8,128)(2,1)S(1)}, bf16[32,5120]{1,0:T(8,128)(2,1)S(1)}, u32[]{:S(2)}, u32[]{:S(2)}) %collective-permute-start.4) | collective-permute-done | bytes 327712 | tf_op jit(solution)/shard_map/ppermute | solution.py:498
  29.7 0.5 collective-permute-start.8
  30.2 1.7 %collective-permute-done.8.a2 = bf16[32,5120]{1,0:T(8,128)(2,1)S(1)} collective-permute-done((bf16[32,5120]{1,0:T(8,128)(2,1)S(1)}, bf16[32,5120]{1,0:T(8,128)(2,1)S(1)}, u32[]{:S(2)}, u32[]{:S(2)}) %collective-permute-start.8) | collective-permute-done | bytes 327712 | tf_op jit(solution)/shard_map/ppermute | solution.py:498
  31.9 0.5 collective-permute-done.9.a3
  32.3 0.5 shard_map.110
  32.9 0.2 collective-permute-start.11
  33.1 1.7 %shard_map.111.acc_ref = f32[128,512]{1,0:T(8,128)S(1)} custom-call(bf16[32,5120]{1,0:T(8,128)(2,1)S(1)} %bitcast.74, bf16[32,5120]{1,0:T(8,128)(2,1)S(1)} %collective-permute-done.4.a1, bf16[32,5120]{1,0:T(8,128)(2,1)S(1)} %collective-permute-done.8.a2, bf16[32,5120]{1,0:T(8,128)(2,1)S(1)} %collective-permute-done.9.a3, bf16[5120,512]{1,0:T(8,128)(2,1)S(1)} %bitcast.63), custom_call_target="tpu_custom_call" | custom-call | flops 671088640 | bytes 6553600 | tf_op jit(solution)/shard_map/pallas_call | solution.py:178
  34.8 0.0 copy-start.1
  34.9 0.1 fusion.6
  35.0 1.5 %collective-permute-start.12 = (bf16[128,512]{1,0:T(8,128)(2,1)S(1)}, bf16[128,512]{1,0:T(8,128)(2,1)S(1)}, u32[]{:S(2)}, u32[]{:S(2)}) collective-permute-start(bf16[128,512]{1,0:T(8,128)(2,1)S(1)} %pad_maximum_fusion.1), channel_id=1, source_target_pairs={{0,2},{1,3},{2,0},{3,1},{4,6},{5,7},{6,4},{7,5},{8,10},{9,11},{10,... | collective-permute-start | bytes 393224 | tf_op jit(solution)/shard_map/ppermute | solution.py:498
  36.5 1.0 shard_map.112
  37.5 3.3 %collective-permute-done.12 = bf16[128,512]{1,0:T(8,128)(2,1)S(1)} collective-permute-done((bf16[128,512]{1,0:T(8,128)(2,1)S(1)}, bf16[128,512]{1,0:T(8,128)(2,1)S(1)}, u32[]{:S(2)}, u32[]{:S(2)}) %collective-permute-start.12) | collective-permute-done | bytes 131104 | tf_op jit(solution)/shard_map/ppermute | solution.py:498
  40.9 0.4 collective-permute-start.13
  41.2 0.7 collective-permute-start.14
  41.9 4.7 %collective-permute-start.16 = (bf16[128,512]{1,0:T(8,128)(2,1)S(1)}, bf16[128,512]{1,0:T(8,128)(2,1)S(1)}, u32[]{:S(2)}, u32[]{:S(2)}) collective-permute-start(bf16[128,512]{1,0:T(8,128)(2,1)S(1)} %shard_map.112), channel_id=1, source_target_pairs={{0,8},{1,0},{2,9},{3,1},{4,10},{5,2},{6,11},{7,3},{8,12},{9,4},{10... | collective-permute-start | bytes 393224 | tf_op jit(solution)/shard_map/ppermute | solution.py:498
  46.6 0.0 slice-start
  46.6 0.0 slice-start.1
  46.7 5.5 %collective-permute-start.15 = (bf16[128,256]{1,0:T(8,128)(2,1)S(1)}, bf16[128,256]{1,0:T(8,128)(2,1)S(1)}, u32[]{:S(2)}, u32[]{:S(2)}) collective-permute-start(bf16[128,256]{1,0:T(8,128)(2,1)S(1)} %convert_element_type.109), channel_id=1, source_target_pairs={{0,8},{1,9},{2,10},{3,11},{4,12},{5,13},{6,14},{7,15},{8,0},{9,1},... | collective-permute-start | bytes 196616 | tf_op jit(solution)/shard_map/ppermute | solution.py:498
  52.2 10.8 %shard_map.113 = (f32[152,8,128]{2,1,0:T(8,128)S(1)}, f32[152,8,128]{2,1,0:T(8,128)S(1)}, f32[152,8,128]{2,1,0:T(8,128)S(1)}) custom-call(s32[12]{0:T(128)S(1)} %copy-done.6, s32[128]{0:T(128)S(1)} %copy-done.5, bf16[128,512]{1,0:T(8,128)(2,1)S(1)} %collective-permute-done.14.refs_0_, bf16[128,512]{1,0:T(8,128)(2,1)S(1)} %collective-permute-done.16.refs_1_, ...), custom_call_target="tpu_custom_call" | custom-call | flops 1189085184 | bytes 22806528 | tf_op jit(solution)/shard_map/pallas_call | solution.py:388
  63.0 3.1 %shard_map.114 = (bf16[128,512]{1,0:T(8,128)(2,1)S(1)}, bf16[128,512]{1,0:T(8,128)(2,1)S(1)}) custom-call(f32[128,256]{1,0:T(8,128)S(1)} %convert_add_fusion.3.kv_ref, f32[128,128]{1,0:T(8,128)S(1)} %get-tuple-element.51.refs_2_.cos_ref, f32[128,128]{1,0:T(8,128)S(1)} %get-tuple-element.52.refs_3_.sin_ref, f32[152,8,128]{2,1,0:T(8,128)S(1)} %get-tuple-element.54.q_ref, ...), custom_call_target="tpu_custom_call" | custom-call | flops 3112960 | bytes 2490368 | tf_op jit(solution)/shard_map/pallas_call | solution.py:367
  66.2 0.7 collective-permute-start.17
  66.9 4.3 %collective-permute-start.18 = (bf16[128,512]{1,0:T(8,128)(2,1)S(1)}, bf16[128,512]{1,0:T(8,128)(2,1)S(1)}, u32[]{:S(2)}, u32[]{:S(2)}) collective-permute-start(bf16[128,512]{1,0:T(8,128)(2,1)S(1)} %get-tuple-element.58), channel_id=1, source_target_pairs={{8,0},{0,1},{9,2},{1,3},{10,4},{2,5},{11,6},{3,7},{12,8},{4,9},{13... | collective-permute-start | bytes 393224 | tf_op jit(solution)/shard_map/ppermute | solution.py:498
  71.2 3.3 %collective-permute-done.18.refs_1_ = bf16[128,512]{1,0:T(8,128)(2,1)S(1)} collective-permute-done((bf16[128,512]{1,0:T(8,128)(2,1)S(1)}, bf16[128,512]{1,0:T(8,128)(2,1)S(1)}, u32[]{:S(2)}, u32[]{:S(2)}) %collective-permute-start.18) | collective-permute-done | bytes 131104 | tf_op jit(solution)/shard_map/ppermute | solution.py:498
  74.6 3.4 %shard_map.115 = (bf16[64,8192]{1,0:T(8,128)(2,1)S(1)}, bf16[64,8192]{1,0:T(8,128)(2,1)S(1)}) custom-call(bf16[128,512]{1,0:T(8,128)(2,1)S(1)} %collective-permute-done.17.refs_0_, bf16[128,512]{1,0:T(8,128)(2,1)S(1)} %collective-permute-done.18.refs_1_, bf16[512,8192]{1,0:T(8,128)(2,1)S(1)} %bitcast.67), custom_call_target="tpu_custom_call" | custom-call | flops 1073741824 | bytes 10485760 | tf_op jit(solution)/shard_map/pallas_call | solution.py:452
  78.0 0.2 collective-permute-start.19
  78.2 2.5 %collective-permute-done.19 = bf16[64,8192]{1,0:T(8,128)(2,1)S(1)} collective-permute-done((bf16[64,8192]{1,0:T(8,128)(2,1)S(1)}, bf16[64,8192]{1,0:T(8,128)(2,1)S(1)}, u32[]{:S(2)}, u32[]{:S(2)}) %collective-permute-start.19) | collective-permute-done | bytes 1048608 | tf_op jit(solution)/shard_map/ppermute | solution.py:498
  80.7 0.1 add_convert_fusion.4
  80.9 4.9 %collective-permute-start.24 = (bf16[2,8,3072]{2,1,0:T(8,128)(2,1)S(1)}, bf16[2,8,3072]{2,1,0:T(8,128)(2,1)S(1)}, u32[]{:S(2)}, u32[]{:S(2)}) collective-permute-start(bf16[2,8,3072]{2,1,0:T(8,128)(2,1)S(1)} %get-tuple-element.67), channel_id=1, source_target_pairs={{0,4},{1,5},{2,6},{3,7},{4,8},{5,9},{6,10},{7,11},{8,12},{9,13},{1... | collective-permute-start | bytes 294920 | tf_op jit(solution)/shard_map/ppermute | solution.py:498
  85.8 1.9 %collective-permute-start.25 = (bf16[2,8,3072]{2,1,0:T(8,128)(2,1)S(1)}, bf16[2,8,3072]{2,1,0:T(8,128)(2,1)S(1)}, u32[]{:S(2)}, u32[]{:S(2)}) collective-permute-start(bf16[2,8,3072]{2,1,0:T(8,128)(2,1)S(1)} %get-tuple-element.68), channel_id=1, source_target_pairs={{0,8},{1,9},{2,10},{3,11},{4,12},{5,13},{6,14},{7,15},{8,0},{9,1},... | collective-permute-start | bytes 294920 | tf_op jit(solution)/shard_map/ppermute | solution.py:498
  87.7 0.5 collective-permute-start.26
  88.2 0.1 add_convert_fusion.1
  88.3 1.4 %collective-permute-start.20 = (bf16[32,5120]{1,0:T(8,128)(2,1)S(1)}, bf16[32,5120]{1,0:T(8,128)(2,1)S(1)}, u32[]{:S(2)}, u32[]{:S(2)}) collective-permute-start(bf16[32,5120]{1,0:T(8,128)(2,1)S(1)} %add_convert_fusion.1), channel_id=1, source_target_pairs={{0,2},{1,3},{2,0},{3,1},{4,6},{5,7},{6,4},{7,5},{8,10},{9,11},{10,... | collective-permute-start | bytes 983048 | tf_op jit(solution)/shard_map/ppermute | solution.py:498
  89.7 1.2 %collective-permute-done.24 = bf16[2,8,3072]{2,1,0:T(8,128)(2,1)S(1)} collective-permute-done((bf16[2,8,3072]{2,1,0:T(8,128)(2,1)S(1)}, bf16[2,8,3072]{2,1,0:T(8,128)(2,1)S(1)}, u32[]{:S(2)}, u32[]{:S(2)}) %collective-permute-start.24) | collective-permute-done | bytes 98336 | tf_op jit(solution)/shard_map/ppermute | solution.py:498
  90.9 3.9 %collective-permute-done.25 = bf16[2,8,3072]{2,1,0:T(8,128)(2,1)S(1)} collective-permute-done((bf16[2,8,3072]{2,1,0:T(8,128)(2,1)S(1)}, bf16[2,8,3072]{2,1,0:T(8,128)(2,1)S(1)}, u32[]{:S(2)}, u32[]{:S(2)}) %collective-permute-start.25) | collective-permute-done | bytes 98336 | tf_op jit(solution)/shard_map/ppermute | solution.py:498
  94.8 1.1 collective-permute-start.27
  95.9 2.3 %collective-permute-done.20 = bf16[32,5120]{1,0:T(8,128)(2,1)S(1)} collective-permute-done((bf16[32,5120]{1,0:T(8,128)(2,1)S(1)}, bf16[32,5120]{1,0:T(8,128)(2,1)S(1)}, u32[]{:S(2)}, u32[]{:S(2)}) %collective-permute-start.20) | collective-permute-done | bytes 327712 | tf_op jit(solution)/shard_map/ppermute | solution.py:498
  98.2 0.1 add_convert_fusion
  98.3 0.9 collective-permute-start.21
  99.2 1.0 collective-permute-start.22
  100.2 2.0 %collective-permute-start.23 = (bf16[8,5120]{1,0:T(8,128)(2,1)S(1)}, bf16[8,5120]{1,0:T(8,128)(2,1)S(1)}, u32[]{:S(2)}, u32[]{:S(2)}) collective-permute-start(bf16[8,5120]{1,0:T(8,128)(2,1)S(1)} %get-tuple-element.71), channel_id=1, source_target_pairs={{0,12},{1,13},{2,14},{3,15},{4,0},{5,1},{6,2},{7,3},{8,4},{9,5},{1... | collective-permute-start | bytes 245768 | tf_op jit(solution)/shard_map/ppermute | solution.py:498
  102.2 2.8 %collective-permute-done.21 = bf16[8,5120]{1,0:T(8,128)(2,1)S(1)} collective-permute-done((bf16[8,5120]{1,0:T(8,128)(2,1)S(1)}, bf16[8,5120]{1,0:T(8,128)(2,1)S(1)}, u32[]{:S(2)}, u32[]{:S(2)}) %collective-permute-start.21) | collective-permute-done | bytes 81952 | tf_op jit(solution)/shard_map/ppermute | solution.py:498
  105.1 2.1 %collective-permute-done.22 = bf16[8,5120]{1,0:T(8,128)(2,1)S(1)} collective-permute-done((bf16[8,5120]{1,0:T(8,128)(2,1)S(1)}, bf16[8,5120]{1,0:T(8,128)(2,1)S(1)}, u32[]{:S(2)}, u32[]{:S(2)}) %collective-permute-start.22) | collective-permute-done | bytes 81952 | tf_op jit(solution)/shard_map/ppermute | solution.py:498
  107.3 0.7 fusion
  (60 shorter events, 0.6 us)
Async XLA Ops:
  0.0 0.9 copy-start.2
  0.9 0.7 copy-start.4
  1.8 13.1 %collective-permute-start = (bf16[8,5120]{1,0:T(8,128)(2,1)S(1)}, bf16[8,5120]{1,0:T(8,128)(2,1)S(1)}, u32[]{:S(2)}, u32[]{:S(2)}) collective-permute-start(bf16[8,5120]{1,0:T(8,128)(2,1)S(1)} %get-tuple-element.33), channel_id=1, source_target_pairs={{0,4},{1,5},{2,6},{3,7},{4,8},{5,9},{6,10},{7,11},{8,12},{9,13},{1... | collective-permute-start | bytes 245768 | tf_op jit(solution)/shard_map/ppermute | solution.py:498
  4.9 10.0 %collective-permute-start.1 = (bf16[8,5120]{1,0:T(8,128)(2,1)S(1)}, bf16[8,5120]{1,0:T(8,128)(2,1)S(1)}, u32[]{:S(2)}, u32[]{:S(2)}) collective-permute-start(bf16[8,5120]{1,0:T(8,128)(2,1)S(1)} %get-tuple-element.33), channel_id=1, source_target_pairs={{0,8},{1,9},{2,10},{3,11},{4,12},{5,13},{6,14},{7,15},{8,0},{9,1},... | collective-permute-start | bytes 245768 | tf_op jit(solution)/shard_map/ppermute | solution.py:498
  7.5 7.5 %collective-permute-start.2 = (bf16[8,5120]{1,0:T(8,128)(2,1)S(1)}, bf16[8,5120]{1,0:T(8,128)(2,1)S(1)}, u32[]{:S(2)}, u32[]{:S(2)}) collective-permute-start(bf16[8,5120]{1,0:T(8,128)(2,1)S(1)} %get-tuple-element.33), channel_id=1, source_target_pairs={{0,12},{1,13},{2,14},{3,15},{4,0},{5,1},{6,2},{7,3},{8,4},{9,5},{1... | collective-permute-start | bytes 245768 | tf_op jit(solution)/shard_map/ppermute | solution.py:498
  8.9 6.0 %collective-permute-start.3 = (bf16[8,3072]{1,0:T(8,128)(2,1)S(1)}, bf16[8,3072]{1,0:T(8,128)(2,1)S(1)}, u32[]{:S(2)}, u32[]{:S(2)}) collective-permute-start(bf16[8,3072]{1,0:T(8,128)(2,1)S(1)} %get-tuple-element.34), channel_id=1, source_target_pairs={{0,2},{1,3},{2,0},{3,1},{4,6},{5,7},{6,4},{7,5},{8,10},{9,11},{10,... | collective-permute-start | bytes 147464 | tf_op jit(solution)/shard_map/ppermute | solution.py:498
  15.0 7.5 %collective-permute-start.5 = (bf16[2,8,3072]{2,1,0:T(8,128)(2,1)S(1)}, bf16[2,8,3072]{2,1,0:T(8,128)(2,1)S(1)}, u32[]{:S(2)}, u32[]{:S(2)}) collective-permute-start(bf16[2,8,3072]{2,1,0:T(8,128)(2,1)S(1)} %pad_maximum_fusion.2), channel_id=1, source_target_pairs={{0,4},{1,5},{2,6},{3,7},{4,8},{5,9},{6,10},{7,11},{8,12},{9,13},{1... | collective-permute-start | bytes 294920 | tf_op jit(solution)/shard_map/ppermute | solution.py:498
  15.8 3.3 %slice-start.2 = ((bf16[8192,4,128]{2,1,0:T(4,128)(2,1)}), bf16[5120,4,128]{2,1,0:T(4,128)(2,1)S(1)}, s32[]{:S(2)}) async-start(bf16[8192,4,128]{2,1,0:T(4,128)(2,1)} %param.13), calls=%async_computation.2 | async-start | bytes 10485760 | tf_op jit(solution)/shard_map/slice | solution.py:527
  15.8 8.8 %collective-permute-start.6 = (bf16[2,8,3072]{2,1,0:T(8,128)(2,1)S(1)}, bf16[2,8,3072]{2,1,0:T(8,128)(2,1)S(1)}, u32[]{:S(2)}, u32[]{:S(2)}) collective-permute-start(bf16[2,8,3072]{2,1,0:T(8,128)(2,1)S(1)} %pad_maximum_fusion.2), channel_id=1, source_target_pairs={{0,8},{1,9},{2,10},{3,11},{4,12},{5,13},{6,14},{7,15},{8,0},{9,1},... | collective-permute-start | bytes 294920 | tf_op jit(solution)/shard_map/ppermute | solution.py:498
  17.3 7.3 %collective-permute-start.7 = (bf16[2,8,3072]{2,1,0:T(8,128)(2,1)S(1)}, bf16[2,8,3072]{2,1,0:T(8,128)(2,1)S(1)}, u32[]{:S(2)}, u32[]{:S(2)}) collective-permute-start(bf16[2,8,3072]{2,1,0:T(8,128)(2,1)S(1)} %pad_maximum_fusion.2), channel_id=1, source_target_pairs={{0,12},{1,13},{2,14},{3,15},{4,0},{5,1},{6,2},{7,3},{8,4},{9,5},{1... | collective-permute-start | bytes 294920 | tf_op jit(solution)/shard_map/ppermute | solution.py:498
  19.1 1.9 %slice-start.3 = ((bf16[8192,4,128]{2,1,0:T(4,128)(2,1)}), bf16[3072,4,128]{2,1,0:T(4,128)(2,1)S(1)}, s32[]{:S(2)}) async-start(bf16[8192,4,128]{2,1,0:T(4,128)(2,1)} %param.13), calls=%async_computation.3 | async-start | bytes 6291456 | tf_op jit(solution)/shard_map/slice | solution.py:528
  21.5 8.2 %collective-permute-start.4 = (bf16[32,5120]{1,0:T(8,128)(2,1)S(1)}, bf16[32,5120]{1,0:T(8,128)(2,1)S(1)}, u32[]{:S(2)}, u32[]{:S(2)}) collective-permute-start(bf16[32,5120]{1,0:T(8,128)(2,1)S(1)} %bitcast.71), channel_id=1, source_target_pairs={{0,2},{1,3},{2,0},{3,1},{4,6},{5,7},{6,4},{7,5},{8,10},{9,11},{10,... | collective-permute-start | bytes 983048 | tf_op jit(solution)/shard_map/ppermute | solution.py:498
  29.7 2.7 %collective-permute-start.10 = (bf16[64,3072]{1,0:T(8,128)(2,1)S(1)}, bf16[64,3072]{1,0:T(8,128)(2,1)S(1)}, u32[]{:S(2)}, u32[]{:S(2)}) collective-permute-start(bf16[64,3072]{1,0:T(8,128)(2,1)S(1)} %bitcast.68), channel_id=1, source_target_pairs={{0,1},{1,0},{2,3},{3,2},{4,5},{5,4},{6,7},{7,6},{8,9},{9,8},{10,11... | collective-permute-start | bytes 1179656 | tf_op jit(solution)/shard_map/ppermute | solution.py:498
  29.7 2.2 %collective-permute-start.8 = (bf16[32,5120]{1,0:T(8,128)(2,1)S(1)}, bf16[32,5120]{1,0:T(8,128)(2,1)S(1)}, u32[]{:S(2)}, u32[]{:S(2)}) collective-permute-start(bf16[32,5120]{1,0:T(8,128)(2,1)S(1)} %bitcast.72), channel_id=1, source_target_pairs={{0,1},{1,0},{2,3},{3,2},{4,5},{5,4},{6,7},{7,6},{8,9},{9,8},{10,11... | collective-permute-start | bytes 983048 | tf_op jit(solution)/shard_map/ppermute | solution.py:498
  30.2 2.1 %collective-permute-start.9 = (bf16[32,5120]{1,0:T(8,128)(2,1)S(1)}, bf16[32,5120]{1,0:T(8,128)(2,1)S(1)}, u32[]{:S(2)}, u32[]{:S(2)}) collective-permute-start(bf16[32,5120]{1,0:T(8,128)(2,1)S(1)} %collective-permute-done.4.a1), channel_id=1, source_target_pairs={{0,1},{1,0},{2,3},{3,2},{4,5},{5,4},{6,7},{7,6},{8,9},{9,8},{10,11... | collective-permute-start | bytes 983048 | tf_op jit(solution)/shard_map/ppermute | solution.py:498
  32.9 1.9 %collective-permute-start.11 = (bf16[128,1024]{1,0:T(8,128)(2,1)S(1)}, bf16[128,1024]{1,0:T(8,128)(2,1)S(1)}, u32[]{:S(2)}, u32[]{:S(2)}) collective-permute-start(bf16[128,1024]{1,0:T(8,128)(2,1)S(1)} %get-tuple-element.43), channel_id=1, source_target_pairs={{0,1},{1,0},{2,3},{3,2},{4,5},{5,4},{6,7},{7,6},{8,9},{9,8},{10,11... | collective-permute-start | bytes 786440 | tf_op jit(solution)/shard_map/ppermute | solution.py:498
  34.8 17.3 %copy-start = (bf16[1,6,2048,128]{3,2,1,0:T(8,128)(2,1)S(1)}, bf16[1,6,2048,128]{3,2,1,0:T(8,128)(2,1)}, u32[]{:S(2)}) copy-start(bf16[1,6,2048,128]{3,2,1,0:T(8,128)(2,1)} %refs_4_.1) | copy-start | bytes 9437188
  34.8 17.3 %copy-start.1 = (bf16[1,6,2048,128]{3,2,1,0:T(8,128)(2,1)S(1)}, bf16[1,6,2048,128]{3,2,1,0:T(8,128)(2,1)}, u32[]{:S(2)}) copy-start(bf16[1,6,2048,128]{3,2,1,0:T(8,128)(2,1)} %refs_5_.1) | copy-start | bytes 9437188
  34.8 17.3 %copy-start.5 = (s32[128]{0:T(128)S(1)}, s32[128]{0:T(128)}, u32[]{:S(2)}) copy-start(s32[128]{0:T(128)} %lens_ref.1) | copy-start | bytes 1540
  34.8 17.3 %copy-start.6 = (s32[12]{0:T(128)S(1)}, s32[12]{0:T(128)}, u32[]{:S(2)}) copy-start(s32[12]{0:T(128)} %counts_ref.1) | copy-start | bytes 148
  35.0 5.9 %collective-permute-start.12 = (bf16[128,512]{1,0:T(8,128)(2,1)S(1)}, bf16[128,512]{1,0:T(8,128)(2,1)S(1)}, u32[]{:S(2)}, u32[]{:S(2)}) collective-permute-start(bf16[128,512]{1,0:T(8,128)(2,1)S(1)} %pad_maximum_fusion.1), channel_id=1, source_target_pairs={{0,2},{1,3},{2,0},{3,1},{4,6},{5,7},{6,4},{7,5},{8,10},{9,11},{10,... | collective-permute-start | bytes 393224 | tf_op jit(solution)/shard_map/ppermute | solution.py:498
  40.9 5.7 %collective-permute-start.13 = (bf16[128,256]{1,0:T(8,128)(2,1)S(1)}, bf16[128,256]{1,0:T(8,128)(2,1)S(1)}, u32[]{:S(2)}, u32[]{:S(2)}) collective-permute-start(bf16[128,256]{1,0:T(8,128)(2,1)S(1)} %slice.155), channel_id=1, source_target_pairs={{0,4},{1,5},{2,6},{3,7},{4,0},{5,1},{6,2},{7,3},{8,12},{9,13},{10,... | collective-permute-start | bytes 196616 | tf_op jit(solution)/shard_map/ppermute | solution.py:498
  41.2 5.4 %collective-permute-start.14 = (bf16[128,512]{1,0:T(8,128)(2,1)S(1)}, bf16[128,512]{1,0:T(8,128)(2,1)S(1)}, u32[]{:S(2)}, u32[]{:S(2)}) collective-permute-start(bf16[128,512]{1,0:T(8,128)(2,1)S(1)} %shard_map.112), channel_id=1, source_target_pairs={{0,0},{1,8},{2,1},{3,9},{4,2},{5,10},{6,3},{7,11},{8,4},{9,12},{10... | collective-permute-start | bytes 393224 | tf_op jit(solution)/shard_map/ppermute | solution.py:498
  41.9 10.2 %collective-permute-start.16 = (bf16[128,512]{1,0:T(8,128)(2,1)S(1)}, bf16[128,512]{1,0:T(8,128)(2,1)S(1)}, u32[]{:S(2)}, u32[]{:S(2)}) collective-permute-start(bf16[128,512]{1,0:T(8,128)(2,1)S(1)} %shard_map.112), channel_id=1, source_target_pairs={{0,8},{1,0},{2,9},{3,1},{4,10},{5,2},{6,11},{7,3},{8,12},{9,4},{10... | collective-permute-start | bytes 393224 | tf_op jit(solution)/shard_map/ppermute | solution.py:498
  46.6 27.9 %slice-start = ((s8[8388608]{0:T(1024)(128)(4,1)}), s8[4194304]{0:T(1024)(128)(4,1)S(1)}, s32[]{:S(2)}) async-start(s8[8388608]{0:T(1024)(128)(4,1)} %bitcast.65), calls=%async_computation | async-start | bytes 8388608
  46.6 27.9 %slice-start.1 = ((s8[8388608]{0:T(1024)(128)(4,1)}), s8[4194304]{0:T(1024)(128)(4,1)S(1)}, s32[]{:S(2)}) async-start(s8[8388608]{0:T(1024)(128)(4,1)} %bitcast.65), calls=%async_computation.1 | async-start | bytes 8388608
  46.7 16.4 %collective-permute-start.15 = (bf16[128,256]{1,0:T(8,128)(2,1)S(1)}, bf16[128,256]{1,0:T(8,128)(2,1)S(1)}, u32[]{:S(2)}, u32[]{:S(2)}) collective-permute-start(bf16[128,256]{1,0:T(8,128)(2,1)S(1)} %convert_element_type.109), channel_id=1, source_target_pairs={{0,8},{1,9},{2,10},{3,11},{4,12},{5,13},{6,14},{7,15},{8,0},{9,1},... | collective-permute-start | bytes 196616 | tf_op jit(solution)/shard_map/ppermute | solution.py:498
  66.2 5.0 %collective-permute-start.17 = (bf16[128,512]{1,0:T(8,128)(2,1)S(1)}, bf16[128,512]{1,0:T(8,128)(2,1)S(1)}, u32[]{:S(2)}, u32[]{:S(2)}) collective-permute-start(bf16[128,512]{1,0:T(8,128)(2,1)S(1)} %get-tuple-element.57), channel_id=1, source_target_pairs={{0,0},{8,1},{1,2},{9,3},{2,4},{10,5},{3,6},{11,7},{4,8},{12,9},{5,... | collective-permute-start | bytes 393224 | tf_op jit(solution)/shard_map/ppermute | solution.py:498
  66.9 7.7 %collective-permute-start.18 = (bf16[128,512]{1,0:T(8,128)(2,1)S(1)}, bf16[128,512]{1,0:T(8,128)(2,1)S(1)}, u32[]{:S(2)}, u32[]{:S(2)}) collective-permute-start(bf16[128,512]{1,0:T(8,128)(2,1)S(1)} %get-tuple-element.58), channel_id=1, source_target_pairs={{8,0},{0,1},{9,2},{1,3},{10,4},{2,5},{11,6},{3,7},{12,8},{4,9},{13... | collective-permute-start | bytes 393224 | tf_op jit(solution)/shard_map/ppermute | solution.py:498
  78.0 29.3 %copy-start.3 = (bf16[8,8192]{1,0:T(8,128)(2,1)S(1)}, bf16[8,8192]{1,0:T(8,128)(2,1)}, u32[]{:S(2)}) copy-start(bf16[8,8192]{1,0:T(8,128)(2,1)} %x_ref.1) | copy-start | bytes 393220
  78.0 2.7 %collective-permute-start.19 = (bf16[64,8192]{1,0:T(8,128)(2,1)S(1)}, bf16[64,8192]{1,0:T(8,128)(2,1)S(1)}, u32[]{:S(2)}, u32[]{:S(2)}) collective-permute-start(bf16[64,8192]{1,0:T(8,128)(2,1)S(1)} %get-tuple-element.60), channel_id=1, source_target_pairs={{0,1},{1,0},{2,3},{3,2},{4,5},{5,4},{6,7},{7,6},{8,9},{9,8},{10,11... | collective-permute-start | bytes 3145736 | tf_op jit(solution)/shard_map/ppermute | solution.py:498
  80.9 10.0 %collective-permute-start.24 = (bf16[2,8,3072]{2,1,0:T(8,128)(2,1)S(1)}, bf16[2,8,3072]{2,1,0:T(8,128)(2,1)S(1)}, u32[]{:S(2)}, u32[]{:S(2)}) collective-permute-start(bf16[2,8,3072]{2,1,0:T(8,128)(2,1)S(1)} %get-tuple-element.67), channel_id=1, source_target_pairs={{0,4},{1,5},{2,6},{3,7},{4,8},{5,9},{6,10},{7,11},{8,12},{9,13},{1... | collective-permute-start | bytes 294920 | tf_op jit(solution)/shard_map/ppermute | solution.py:498
  85.8 9.0 %collective-permute-start.25 = (bf16[2,8,3072]{2,1,0:T(8,128)(2,1)S(1)}, bf16[2,8,3072]{2,1,0:T(8,128)(2,1)S(1)}, u32[]{:S(2)}, u32[]{:S(2)}) collective-permute-start(bf16[2,8,3072]{2,1,0:T(8,128)(2,1)S(1)} %get-tuple-element.68), channel_id=1, source_target_pairs={{0,8},{1,9},{2,10},{3,11},{4,12},{5,13},{6,14},{7,15},{8,0},{9,1},... | collective-permute-start | bytes 294920 | tf_op jit(solution)/shard_map/ppermute | solution.py:498
  87.7 7.1 %collective-permute-start.26 = (bf16[2,8,3072]{2,1,0:T(8,128)(2,1)S(1)}, bf16[2,8,3072]{2,1,0:T(8,128)(2,1)S(1)}, u32[]{:S(2)}, u32[]{:S(2)}) collective-permute-start(bf16[2,8,3072]{2,1,0:T(8,128)(2,1)S(1)} %get-tuple-element.69), channel_id=1, source_target_pairs={{0,12},{1,13},{2,14},{3,15},{4,0},{5,1},{6,2},{7,3},{8,4},{9,5},{1... | collective-permute-start | bytes 294920 | tf_op jit(solution)/shard_map/ppermute | solution.py:498
  88.3 9.9 %collective-permute-start.20 = (bf16[32,5120]{1,0:T(8,128)(2,1)S(1)}, bf16[32,5120]{1,0:T(8,128)(2,1)S(1)}, u32[]{:S(2)}, u32[]{:S(2)}) collective-permute-start(bf16[32,5120]{1,0:T(8,128)(2,1)S(1)} %add_convert_fusion.1), channel_id=1, source_target_pairs={{0,2},{1,3},{2,0},{3,1},{4,6},{5,7},{6,4},{7,5},{8,10},{9,11},{10,... | collective-permute-start | bytes 983048 | tf_op jit(solution)/shard_map/ppermute | solution.py:498
  94.8 7.4 %collective-permute-start.27 = (bf16[8,3072]{1,0:T(8,128)(2,1)S(1)}, bf16[8,3072]{1,0:T(8,128)(2,1)S(1)}, u32[]{:S(2)}, u32[]{:S(2)}) collective-permute-start(bf16[8,3072]{1,0:T(8,128)(2,1)S(1)} %fusion.4), channel_id=1, source_target_pairs={{0,2},{1,3},{2,0},{3,1},{4,6},{5,7},{6,4},{7,5},{8,10},{9,11},{10,... | collective-permute-start | bytes 147464 | tf_op jit(solution)/shard_map/ppermute | solution.py:498
  98.3 6.7 %collective-permute-start.21 = (bf16[8,5120]{1,0:T(8,128)(2,1)S(1)}, bf16[8,5120]{1,0:T(8,128)(2,1)S(1)}, u32[]{:S(2)}, u32[]{:S(2)}) collective-permute-start(bf16[8,5120]{1,0:T(8,128)(2,1)S(1)} %get-tuple-element.70), channel_id=1, source_target_pairs={{0,4},{1,5},{2,6},{3,7},{4,8},{5,9},{6,10},{7,11},{8,12},{9,13},{1... | collective-permute-start | bytes 245768 | tf_op jit(solution)/shard_map/ppermute | solution.py:498
  99.2 8.0 %collective-permute-start.22 = (bf16[8,5120]{1,0:T(8,128)(2,1)S(1)}, bf16[8,5120]{1,0:T(8,128)(2,1)S(1)}, u32[]{:S(2)}, u32[]{:S(2)}) collective-permute-start(bf16[8,5120]{1,0:T(8,128)(2,1)S(1)} %get-tuple-element.72), channel_id=1, source_target_pairs={{0,8},{1,9},{2,10},{3,11},{4,12},{5,13},{6,14},{7,15},{8,0},{9,1},... | collective-permute-start | bytes 245768 | tf_op jit(solution)/shard_map/ppermute | solution.py:498
  100.2 7.0 %collective-permute-start.23 = (bf16[8,5120]{1,0:T(8,128)(2,1)S(1)}, bf16[8,5120]{1,0:T(8,128)(2,1)S(1)}, u32[]{:S(2)}, u32[]{:S(2)}) collective-permute-start(bf16[8,5120]{1,0:T(8,128)(2,1)S(1)} %get-tuple-element.71), channel_id=1, source_target_pairs={{0,12},{1,13},{2,14},{3,15},{4,0},{5,1},{6,2},{7,3},{8,4},{9,5},{1... | collective-permute-start | bytes 245768 | tf_op jit(solution)/shard_map/ppermute | solution.py:498

commit v2 on v1

--- a/solution.py
+++ b/solution.py
@@ -442,11 +442,11 @@
     send_ref[...] = value[half:]
 
 
-def output_product(parts, w):
+def output_product(parts, w, first, cols):
     groups = len(parts)
     rows, share = parts[0].shape
-    cols = w.shape[1]
     block = 1024
+    skip = first // block
     zn = rows // (8 * CORES * SIDE)
     half = rows // 2
     return pl.pallas_call(
@@ -454,7 +454,7 @@
         grid=(cols // block,),
         out_shape=(jax.ShapeDtypeStruct((half, cols), BF16),) * 2,
         in_specs=[pl.BlockSpec((rows, share), lambda i: (0, 0)) for _ in parts]
-        + [pl.BlockSpec((share, block), lambda i: (0, i))],
+        + [pl.BlockSpec((share, block), lambda i: (0, i + skip))],
         out_specs=(pl.BlockSpec((half, block), lambda i: (0, i)),) * 2,
         scratch_shapes=[
             pltpu.VMEM((zn, SIDE, CORES, 8, share), F32),
@@ -593,20 +593,23 @@
         )
         for k in range(groups)
     ]
-    keep, send = output_product(parts, w_out.reshape(hs * hd, w_out.shape[2]))
-    came = swap(send, 1)
+    weight = w_out.reshape(hs * hd, width_all)
+    far_keep, far_send = output_product(parts, weight, cut, width_all - cut)
+    far_came = swap(far_send, 1)
+    parts[0], far_keep = lax.optimization_barrier((parts[0], far_keep))
+    near_keep, near_send = output_product(parts, weight, 0, cut)
+    near_came = swap(near_send, 1)
     part = zn * local_rows
 
-    def pair_sum(first, last):
-        return (keep[first[0] : first[1], last].astype(F32) + came[first[0] : first[1], last].astype(F32))
-
-    own, other = (0, part), (part, 2 * part)
-    near_cols, far_cols = slice(0, cut), slice(cut, width_all)
-    near_go = swap(pair_sum(other, near_cols).astype(BF16), CORES)
-    far_all = jnp.concatenate([pair_sum(own, far_cols), pair_sum(other, far_cols)], 0)
+    def pair_sum(keep, came, first):
+        rows = slice(first, first + part)
+        return keep[rows].astype(F32) + came[rows].astype(F32)
+
+    near_go = swap(pair_sum(near_keep, near_came, part).astype(BF16), CORES)
+    far_all = far_keep.astype(F32) + far_came.astype(F32)
     far_all = far_all.astype(BF16).reshape(SIDE, zn, local_rows, width_all - cut)
     far_moved = [shift(far_all[:, k], k) for k in range(1, zn)]
-    near_sum = pair_sum(own, near_cols).astype(BF16).astype(F32) + near_go.astype(F32)
+    near_sum = pair_sum(near_keep, near_came, 0).astype(BF16).astype(F32) + near_go.astype(F32)
     near_all = near_sum.astype(BF16).reshape(zn, local_rows, cut)
     near_moved = [shift(near_all[k], k) for k in range(1, zn)]
     far_sum = far_all[:, 0].astype(F32)

time: 108 us -> 113 us (1.046)
  waiting for transfers between devices: 31.2 us -> 34.7 us
    ppermute x28 -> x29, waiting for transfers between devices: 31.2 us -> 34.7 us  [move(): return lax.ppermute(x, 'tensor', pairs)]
    ppermute x28 -> x29, starting transfers between devices: 45.3 us -> 46.3 us  [move(): return lax.ppermute(x, 'tensor', pairs)]
    pallas_call x1 -> x2, Pallas kernels: 3.42 us -> 3.51 us  [output_product(): pl.pallas_call(functools.partial(output_kernel, groups, zn), grid=(cols /...]
  transfers between devices with their start and end apart: 28 -> 29, of which waited for: 13 -> 13; matrix products, arithmetic and copies ran while one was open for 6% -> 6% of each run, Pallas kernels for 13% -> 14%
where the time goes in v2:
time: 113 us
  starting transfers between devices  46.3 us (41%)
  waiting for transfers between devices  34.7 us (31%)
  Pallas kernels  21 us (19%)
  local copies, waits for them, and re-layouts  7.64 us (7%)
  other arithmetic  2.34 us (2%)
    ppermute x29, starting transfers between devices, move(): return lax.ppermute(x, 'tensor', pairs)  46.3 us
    ppermute x29, waiting for transfers between devices, move(): return lax.ppermute(x, 'tensor', pairs)  34.7 us
    pallas_call x1, Pallas kernels, attend(): pl.pallas_call(functools.partial(attend_kernel, groups, kvh, hs), out_sha...  10.8 us
    pallas_call x2, Pallas kernels, output_product(): pl.pallas_call(functools.partial(output_kernel, groups, zn), grid=(cols /...  3.51 us
    reshape x1, local copies, waits for them, and re-layouts, local(): wkv = w_kv.reshape(slab, kvh * 2 * hd)  3.3 us
    pallas_call x1, Pallas kernels, merge(): pl.pallas_call(functools.partial(merge_kernel, groups, kvh), out_shape=tu...  3.15 us
    unnamed x20, local copies, waits for them, and re-layouts  3.11 us
  transfers between devices with their start and end apart: 29, of which 13 were waited for; matrix products, arithmetic and copies ran while one was open for 6% of the time, Pallas kernels for 14%

profile of v2, /device:TPU:0, one launch (start us, length us, event | category | flops | bytes accessed | tf_op | source)
XLA Modules:
  0.0 112.6 jit_solution(6540530075528114407)
XLA Ops:
  0.0 0.9 copy-done.2
  0.9 0.7 copy-done.4
  1.6 0.2 shard_map.109
  1.8 3.1 %collective-permute-start = (bf16[8,5120]{1,0:T(8,128)(2,1)S(1)}, bf16[8,5120]{1,0:T(8,128)(2,1)S(1)}, u32[]{:S(2)}, u32[]{:S(2)}) collective-permute-start(bf16[8,5120]{1,0:T(8,128)(2,1)S(1)} %get-tuple-element.37), channel_id=1, source_target_pairs={{0,4},{1,5},{2,6},{3,7},{4,8},{5,9},{6,10},{7,11},{8,12},{9,13},{1... | collective-permute-start | bytes 245768 | tf_op jit(solution)/shard_map/ppermute | solution.py:498
  4.9 2.6 %collective-permute-start.1 = (bf16[8,5120]{1,0:T(8,128)(2,1)S(1)}, bf16[8,5120]{1,0:T(8,128)(2,1)S(1)}, u32[]{:S(2)}, u32[]{:S(2)}) collective-permute-start(bf16[8,5120]{1,0:T(8,128)(2,1)S(1)} %get-tuple-element.37), channel_id=1, source_target_pairs={{0,8},{1,9},{2,10},{3,11},{4,12},{5,13},{6,14},{7,15},{8,0},{9,1},... | collective-permute-start | bytes 245768 | tf_op jit(solution)/shard_map/ppermute | solution.py:498
  7.5 1.3 %collective-permute-start.2 = (bf16[8,5120]{1,0:T(8,128)(2,1)S(1)}, bf16[8,5120]{1,0:T(8,128)(2,1)S(1)}, u32[]{:S(2)}, u32[]{:S(2)}) collective-permute-start(bf16[8,5120]{1,0:T(8,128)(2,1)S(1)} %get-tuple-element.37), channel_id=1, source_target_pairs={{0,12},{1,13},{2,14},{3,15},{4,0},{5,1},{6,2},{7,3},{8,4},{9,5},{1... | collective-permute-start | bytes 245768 | tf_op jit(solution)/shard_map/ppermute | solution.py:498
  8.9 1.5 %collective-permute-start.3 = (bf16[8,3072]{1,0:T(8,128)(2,1)S(1)}, bf16[8,3072]{1,0:T(8,128)(2,1)S(1)}, u32[]{:S(2)}, u32[]{:S(2)}) collective-permute-start(bf16[8,3072]{1,0:T(8,128)(2,1)S(1)} %get-tuple-element.38), channel_id=1, source_target_pairs={{0,2},{1,3},{2,0},{3,1},{4,6},{5,7},{6,4},{7,5},{8,10},{9,11},{10,... | collective-permute-start | bytes 147464 | tf_op jit(solution)/shard_map/ppermute | solution.py:498
  10.4 0.7 add_convert_fusion.4
  11.1 0.3 fusion.5
  11.4 0.1 pad_maximum_fusion.2
  11.6 3.3 %reshape.41.wkv_ref = bf16[512,2048]{1,0:T(8,128)(2,1)S(1)} reshape(bf16[512,8,2,128]{3,2,1,0:T(2,128)(2,1)} %param.14) | data formatting | bytes 4194304 | tf_op jit(solution)/shard_map/reshape | solution.py:506
  15.0 0.7 collective-permute-start.5
  15.8 0.0 slice-start.2
  15.8 1.5 %collective-permute-start.6 = (bf16[2,8,3072]{2,1,0:T(8,128)(2,1)S(1)}, bf16[2,8,3072]{2,1,0:T(8,128)(2,1)S(1)}, u32[]{:S(2)}, u32[]{:S(2)}) collective-permute-start(bf16[2,8,3072]{2,1,0:T(8,128)(2,1)S(1)} %pad_maximum_fusion.1), channel_id=1, source_target_pairs={{0,8},{1,9},{2,10},{3,11},{4,12},{5,13},{6,14},{7,15},{8,0},{9,1},... | collective-permute-start | bytes 294920 | tf_op jit(solution)/shard_map/ppermute | solution.py:498
  17.3 1.8 %collective-permute-start.7 = (bf16[2,8,3072]{2,1,0:T(8,128)(2,1)S(1)}, bf16[2,8,3072]{2,1,0:T(8,128)(2,1)S(1)}, u32[]{:S(2)}, u32[]{:S(2)}) collective-permute-start(bf16[2,8,3072]{2,1,0:T(8,128)(2,1)S(1)} %pad_maximum_fusion.1), channel_id=1, source_target_pairs={{0,12},{1,13},{2,14},{3,15},{4,0},{5,1},{6,2},{7,3},{8,4},{9,5},{1... | collective-permute-start | bytes 294920 | tf_op jit(solution)/shard_map/ppermute | solution.py:498
  19.1 0.9 copy.32
  20.0 1.0 slice-done.3
  21.0 0.5 copy.33
  21.5 0.6 collective-permute-start.4
  22.1 0.4 collective-permute-done.5
  22.5 2.1 %collective-permute-done.6 = bf16[2,8,3072]{2,1,0:T(8,128)(2,1)S(1)} collective-permute-done((bf16[2,8,3072]{2,1,0:T(8,128)(2,1)S(1)}, bf16[2,8,3072]{2,1,0:T(8,128)(2,1)S(1)}, u32[]{:S(2)}, u32[]{:S(2)}) %collective-permute-start.6) | collective-permute-done | bytes 98336 | tf_op jit(solution)/shard_map/ppermute | solution.py:498
  24.6 5.1 %collective-permute-done.4.a1 = bf16[32,5120]{1,0:T(8,128)(2,1)S(1)} collective-permute-done((bf16[32,5120]{1,0:T(8,128)(2,1)S(1)}, bf16[32,5120]{1,0:T(8,128)(2,1)S(1)}, u32[]{:S(2)}, u32[]{:S(2)}) %collective-permute-start.4) | collective-permute-done | bytes 327712 | tf_op jit(solution)/shard_map/ppermute | solution.py:498
  29.7 0.5 collective-permute-start.8
  30.2 1.7 %collective-permute-done.8.a2 = bf16[32,5120]{1,0:T(8,128)(2,1)S(1)} collective-permute-done((bf16[32,5120]{1,0:T(8,128)(2,1)S(1)}, bf16[32,5120]{1,0:T(8,128)(2,1)S(1)}, u32[]{:S(2)}, u32[]{:S(2)}) %collective-permute-start.8) | collective-permute-done | bytes 327712 | tf_op jit(solution)/shard_map/ppermute | solution.py:498
  31.9 0.5 collective-permute-done.9.a3
  32.3 0.5 shard_map.110
  32.9 0.2 collective-permute-start.11
  33.1 1.7 %shard_map.111.acc_ref = f32[128,512]{1,0:T(8,128)S(1)} custom-call(bf16[32,5120]{1,0:T(8,128)(2,1)S(1)} %bitcast.75, bf16[32,5120]{1,0:T(8,128)(2,1)S(1)} %collective-permute-done.4.a1, bf16[32,5120]{1,0:T(8,128)(2,1)S(1)} %collective-permute-done.8.a2, bf16[32,5120]{1,0:T(8,128)(2,1)S(1)} %collective-permute-done.9.a3, bf16[5120,512]{1,0:T(8,128)(2,1)S(1)} %bitcast.67), custom_call_target="tpu_custom_call" | custom-call | flops 671088640 | bytes 6553600 | tf_op jit(solution)/shard_map/pallas_call | solution.py:178
  34.9 0.1 fusion.6
  35.0 1.5 %collective-permute-start.12 = (bf16[128,512]{1,0:T(8,128)(2,1)S(1)}, bf16[128,512]{1,0:T(8,128)(2,1)S(1)}, u32[]{:S(2)}, u32[]{:S(2)}) collective-permute-start(bf16[128,512]{1,0:T(8,128)(2,1)S(1)} %pad_maximum_fusion), channel_id=1, source_target_pairs={{0,2},{1,3},{2,0},{3,1},{4,6},{5,7},{6,4},{7,5},{8,10},{9,11},{10,... | collective-permute-start | bytes 393224 | tf_op jit(solution)/shard_map/ppermute | solution.py:498
  36.5 1.0 shard_map.112
  37.5 3.3 %collective-permute-done.12 = bf16[128,512]{1,0:T(8,128)(2,1)S(1)} collective-permute-done((bf16[128,512]{1,0:T(8,128)(2,1)S(1)}, bf16[128,512]{1,0:T(8,128)(2,1)S(1)}, u32[]{:S(2)}, u32[]{:S(2)}) %collective-permute-start.12) | collective-permute-done | bytes 131104 | tf_op jit(solution)/shard_map/ppermute | solution.py:498
  40.9 0.4 collective-permute-start.13
  41.2 0.7 collective-permute-start.14
  41.9 4.7 %collective-permute-start.16 = (bf16[128,512]{1,0:T(8,128)(2,1)S(1)}, bf16[128,512]{1,0:T(8,128)(2,1)S(1)}, u32[]{:S(2)}, u32[]{:S(2)}) collective-permute-start(bf16[128,512]{1,0:T(8,128)(2,1)S(1)} %shard_map.112), channel_id=1, source_target_pairs={{0,8},{1,0},{2,9},{3,1},{4,10},{5,2},{6,11},{7,3},{8,12},{9,4},{10... | collective-permute-start | bytes 393224 | tf_op jit(solution)/shard_map/ppermute | solution.py:498
  46.6 0.0 slice-start.1
  46.7 5.5 %collective-permute-start.15 = (bf16[128,256]{1,0:T(8,128)(2,1)S(1)}, bf16[128,256]{1,0:T(8,128)(2,1)S(1)}, u32[]{:S(2)}, u32[]{:S(2)}) collective-permute-start(bf16[128,256]{1,0:T(8,128)(2,1)S(1)} %convert_element_type.101), channel_id=1, source_target_pairs={{0,8},{1,9},{2,10},{3,11},{4,12},{5,13},{6,14},{7,15},{8,0},{9,1},... | collective-permute-start | bytes 196616 | tf_op jit(solution)/shard_map/ppermute | solution.py:498
  52.2 10.8 %shard_map.113 = (f32[152,8,128]{2,1,0:T(8,128)S(1)}, f32[152,8,128]{2,1,0:T(8,128)S(1)}, f32[152,8,128]{2,1,0:T(8,128)S(1)}) custom-call(s32[12]{0:T(128)S(1)} %copy-done.6, s32[128]{0:T(128)S(1)} %copy-done.5, bf16[128,512]{1,0:T(8,128)(2,1)S(1)} %collective-permute-done.14.refs_0_, bf16[128,512]{1,0:T(8,128)(2,1)S(1)} %collective-permute-done.16.refs_1_, ...), custom_call_target="tpu_custom_call" | custom-call | flops 1189085184 | bytes 22806528 | tf_op jit(solution)/shard_map/pallas_call | solution.py:388
  63.0 3.1 %shard_map.114 = (bf16[128,512]{1,0:T(8,128)(2,1)S(1)}, bf16[128,512]{1,0:T(8,128)(2,1)S(1)}) custom-call(f32[128,256]{1,0:T(8,128)S(1)} %convert_add_fusion.3.kv_ref, f32[128,128]{1,0:T(8,128)S(1)} %get-tuple-element.55.refs_2_.cos_ref, f32[128,128]{1,0:T(8,128)S(1)} %get-tuple-element.56.refs_3_.sin_ref, f32[152,8,128]{2,1,0:T(8,128)S(1)} %get-tuple-element.58.q_ref, ...), custom_call_target="tpu_custom_call" | custom-call | flops 3112960 | bytes 2490368 | tf_op jit(solution)/shard_map/pallas_call | solution.py:367
  66.2 0.7 collective-permute-start.17
  66.9 4.3 %collective-permute-start.18 = (bf16[128,512]{1,0:T(8,128)(2,1)S(1)}, bf16[128,512]{1,0:T(8,128)(2,1)S(1)}, u32[]{:S(2)}, u32[]{:S(2)}) collective-permute-start(bf16[128,512]{1,0:T(8,128)(2,1)S(1)} %get-tuple-element.62), channel_id=1, source_target_pairs={{8,0},{0,1},{9,2},{1,3},{10,4},{2,5},{11,6},{3,7},{12,8},{4,9},{13... | collective-permute-start | bytes 393224 | tf_op jit(solution)/shard_map/ppermute | solution.py:498
  71.2 3.3 %collective-permute-done.18.refs_1_ = bf16[128,512]{1,0:T(8,128)(2,1)S(1)} collective-permute-done((bf16[128,512]{1,0:T(8,128)(2,1)S(1)}, bf16[128,512]{1,0:T(8,128)(2,1)S(1)}, u32[]{:S(2)}, u32[]{:S(2)}) %collective-permute-start.18) | collective-permute-done | bytes 131104 | tf_op jit(solution)/shard_map/ppermute | solution.py:498
  74.6 1.3 %shard_map.115 = (bf16[64,3072]{1,0:T(8,128)(2,1)S(1)}, bf16[64,3072]{1,0:T(8,128)(2,1)S(1)}) custom-call(bf16[128,512]{1,0:T(8,128)(2,1)S(1)} %collective-permute-done.17.refs_0_, bf16[128,512]{1,0:T(8,128)(2,1)S(1)} %collective-permute-done.18.refs_1_, bf16[512,8192]{1,0:T(8,128)(2,1)S(1)} %bitcast.65), custom_call_target="tpu_custom_call" | custom-call | flops 402653184 | bytes 3932160 | tf_op jit(solution)/shard_map/pallas_call | solution.py:452
  75.9 0.2 collective-permute-start.24
  76.1 1.6 %collective-permute-done.24 = bf16[64,3072]{1,0:T(8,128)(2,1)S(1)} collective-permute-done((bf16[64,3072]{1,0:T(8,128)(2,1)S(1)}, bf16[64,3072]{1,0:T(8,128)(2,1)S(1)}, u32[]{:S(2)}, u32[]{:S(2)}) %collective-permute-start.24) | collective-permute-done | bytes 393248 | tf_op jit(solution)/shard_map/ppermute | solution.py:498
  77.7 0.1 add_convert_fusion
  77.8 4.9 %collective-permute-start.25 = (bf16[2,8,3072]{2,1,0:T(8,128)(2,1)S(1)}, bf16[2,8,3072]{2,1,0:T(8,128)(2,1)S(1)}, u32[]{:S(2)}, u32[]{:S(2)}) collective-permute-start(bf16[2,8,3072]{2,1,0:T(8,128)(2,1)S(1)} %get-tuple-element.73), channel_id=1, source_target_pairs={{0,4},{1,5},{2,6},{3,7},{4,8},{5,9},{6,10},{7,11},{8,12},{9,13},{1... | collective-permute-start | bytes 294920 | tf_op jit(solution)/shard_map/ppermute | solution.py:498
  82.7 1.9 %collective-permute-start.26 = (bf16[2,8,3072]{2,1,0:T(8,128)(2,1)S(1)}, bf16[2,8,3072]{2,1,0:T(8,128)(2,1)S(1)}, u32[]{:S(2)}, u32[]{:S(2)}) collective-permute-start(bf16[2,8,3072]{2,1,0:T(8,128)(2,1)S(1)} %get-tuple-element.74), channel_id=1, source_target_pairs={{0,8},{1,9},{2,10},{3,11},{4,12},{5,13},{6,14},{7,15},{8,0},{9,1},... | collective-permute-start | bytes 294920 | tf_op jit(solution)/shard_map/ppermute | solution.py:498
  84.7 0.5 collective-permute-start.27
  85.2 2.2 %shard_map.116 = (bf16[64,5120]{1,0:T(8,128)(2,1)S(1)}, bf16[64,5120]{1,0:T(8,128)(2,1)S(1)}) custom-call(bf16[128,512]{1,0:T(8,128)(2,1)S(1)} %collective-permute-done.17.refs_0_, bf16[128,512]{1,0:T(8,128)(2,1)S(1)} %collective-permute-done.18.refs_1_, bf16[512,8192]{1,0:T(8,128)(2,1)S(1)} %bitcast.66), custom_call_target="tpu_custom_call" | custom-call | flops 671088640 | bytes 6553600 | tf_op jit(solution)/shard_map/pallas_call | solution.py:452
  87.4 0.1 collective-permute-start.19
  87.4 0.4 collective-permute-done.25
  87.8 3.9 %collective-permute-done.26 = bf16[2,8,3072]{2,1,0:T(8,128)(2,1)S(1)} collective-permute-done((bf16[2,8,3072]{2,1,0:T(8,128)(2,1)S(1)}, bf16[2,8,3072]{2,1,0:T(8,128)(2,1)S(1)}, u32[]{:S(2)}, u32[]{:S(2)}) %collective-permute-start.26) | collective-permute-done | bytes 98336 | tf_op jit(solution)/shard_map/ppermute | solution.py:498
  91.8 0.1 add_convert_fusion.2
  91.9 1.1 collective-permute-start.20
  92.9 1.0 collective-permute-start.28
  94.0 8.1 %collective-permute-done.20 = bf16[32,5120]{1,0:T(8,128)(2,1)S(1)} collective-permute-done((bf16[32,5120]{1,0:T(8,128)(2,1)S(1)}, bf16[32,5120]{1,0:T(8,128)(2,1)S(1)}, u32[]{:S(2)}, u32[]{:S(2)}) %collective-permute-start.20) | collective-permute-done | bytes 327712 | tf_op jit(solution)/shard_map/ppermute | solution.py:498
  102.0 0.1 add_convert_fusion.1
  102.2 2.7 %collective-permute-start.21 = (bf16[8,5120]{1,0:T(8,128)(2,1)S(1)}, bf16[8,5120]{1,0:T(8,128)(2,1)S(1)}, u32[]{:S(2)}, u32[]{:S(2)}) collective-permute-start(bf16[8,5120]{1,0:T(8,128)(2,1)S(1)} %get-tuple-element.76), channel_id=1, source_target_pairs={{0,4},{1,5},{2,6},{3,7},{4,8},{5,9},{6,10},{7,11},{8,12},{9,13},{1... | collective-permute-start | bytes 245768 | tf_op jit(solution)/shard_map/ppermute | solution.py:498
  104.9 0.8 collective-permute-start.22
  105.7 1.7 %collective-permute-start.23 = (bf16[8,5120]{1,0:T(8,128)(2,1)S(1)}, bf16[8,5120]{1,0:T(8,128)(2,1)S(1)}, u32[]{:S(2)}, u32[]{:S(2)}) collective-permute-start(bf16[8,5120]{1,0:T(8,128)(2,1)S(1)} %get-tuple-element.77), channel_id=1, source_target_pairs={{0,12},{1,13},{2,14},{3,15},{4,0},{5,1},{6,2},{7,3},{8,4},{9,5},{1... | collective-permute-start | bytes 245768 | tf_op jit(solution)/shard_map/ppermute | solution.py:498
  107.4 1.6 %collective-permute-done.21 = bf16[8,5120]{1,0:T(8,128)(2,1)S(1)} collective-permute-done((bf16[8,5120]{1,0:T(8,128)(2,1)S(1)}, bf16[8,5120]{1,0:T(8,128)(2,1)S(1)}, u32[]{:S(2)}, u32[]{:S(2)}) %collective-permute-start.21) | collective-permute-done | bytes 81952 | tf_op jit(solution)/shard_map/ppermute | solution.py:498
  109.0 2.8 %collective-permute-done.22 = bf16[8,5120]{1,0:T(8,128)(2,1)S(1)} collective-permute-done((bf16[8,5120]{1,0:T(8,128)(2,1)S(1)}, bf16[8,5120]{1,0:T(8,128)(2,1)S(1)}, u32[]{:S(2)}, u32[]{:S(2)}) %collective-permute-start.22) | collective-permute-done | bytes 81952 | tf_op jit(solution)/shard_map/ppermute | solution.py:498
  111.9 0.7 fusion
  (62 shorter events, 0.5 us)
Async XLA Ops:
  0.0 0.9 copy-start.2
  0.9 0.7 copy-start.4
  1.8 13.1 %collective-permute-start = (bf16[8,5120]{1,0:T(8,128)(2,1)S(1)}, bf16[8,5120]{1,0:T(8,128)(2,1)S(1)}, u32[]{:S(2)}, u32[]{:S(2)}) collective-permute-start(bf16[8,5120]{1,0:T(8,128)(2,1)S(1)} %get-tuple-element.37), channel_id=1, source_target_pairs={{0,4},{1,5},{2,6},{3,7},{4,8},{5,9},{6,10},{7,11},{8,12},{9,13},{1... | collective-permute-start | bytes 245768 | tf_op jit(solution)/shard_map/ppermute | solution.py:498
  4.9 10.0 %collective-permute-start.1 = (bf16[8,5120]{1,0:T(8,128)(2,1)S(1)}, bf16[8,5120]{1,0:T(8,128)(2,1)S(1)}, u32[]{:S(2)}, u32[]{:S(2)}) collective-permute-start(bf16[8,5120]{1,0:T(8,128)(2,1)S(1)} %get-tuple-element.37), channel_id=1, source_target_pairs={{0,8},{1,9},{2,10},{3,11},{4,12},{5,13},{6,14},{7,15},{8,0},{9,1},... | collective-permute-start | bytes 245768 | tf_op jit(solution)/shard_map/ppermute | solution.py:498
  7.5 7.5 %collective-permute-start.2 = (bf16[8,5120]{1,0:T(8,128)(2,1)S(1)}, bf16[8,5120]{1,0:T(8,128)(2,1)S(1)}, u32[]{:S(2)}, u32[]{:S(2)}) collective-permute-start(bf16[8,5120]{1,0:T(8,128)(2,1)S(1)} %get-tuple-element.37), channel_id=1, source_target_pairs={{0,12},{1,13},{2,14},{3,15},{4,0},{5,1},{6,2},{7,3},{8,4},{9,5},{1... | collective-permute-start | bytes 245768 | tf_op jit(solution)/shard_map/ppermute | solution.py:498
  8.9 6.0 %collective-permute-start.3 = (bf16[8,3072]{1,0:T(8,128)(2,1)S(1)}, bf16[8,3072]{1,0:T(8,128)(2,1)S(1)}, u32[]{:S(2)}, u32[]{:S(2)}) collective-permute-start(bf16[8,3072]{1,0:T(8,128)(2,1)S(1)} %get-tuple-element.38), channel_id=1, source_target_pairs={{0,2},{1,3},{2,0},{3,1},{4,6},{5,7},{6,4},{7,5},{8,10},{9,11},{10,... | collective-permute-start | bytes 147464 | tf_op jit(solution)/shard_map/ppermute | solution.py:498
  15.0 7.5 %collective-permute-start.5 = (bf16[2,8,3072]{2,1,0:T(8,128)(2,1)S(1)}, bf16[2,8,3072]{2,1,0:T(8,128)(2,1)S(1)}, u32[]{:S(2)}, u32[]{:S(2)}) collective-permute-start(bf16[2,8,3072]{2,1,0:T(8,128)(2,1)S(1)} %pad_maximum_fusion.1), channel_id=1, source_target_pairs={{0,4},{1,5},{2,6},{3,7},{4,8},{5,9},{6,10},{7,11},{8,12},{9,13},{1... | collective-permute-start | bytes 294920 | tf_op jit(solution)/shard_map/ppermute | solution.py:498
  15.8 3.3 %slice-start.2 = ((bf16[8192,4,128]{2,1,0:T(4,128)(2,1)}), bf16[5120,4,128]{2,1,0:T(4,128)(2,1)S(1)}, s32[]{:S(2)}) async-start(bf16[8192,4,128]{2,1,0:T(4,128)(2,1)} %param.13), calls=%async_computation.2 | async-start | bytes 10485760 | tf_op jit(solution)/shard_map/slice | solution.py:527
  15.8 8.8 %collective-permute-start.6 = (bf16[2,8,3072]{2,1,0:T(8,128)(2,1)S(1)}, bf16[2,8,3072]{2,1,0:T(8,128)(2,1)S(1)}, u32[]{:S(2)}, u32[]{:S(2)}) collective-permute-start(bf16[2,8,3072]{2,1,0:T(8,128)(2,1)S(1)} %pad_maximum_fusion.1), channel_id=1, source_target_pairs={{0,8},{1,9},{2,10},{3,11},{4,12},{5,13},{6,14},{7,15},{8,0},{9,1},... | collective-permute-start | bytes 294920 | tf_op jit(solution)/shard_map/ppermute | solution.py:498
  17.3 7.3 %collective-permute-start.7 = (bf16[2,8,3072]{2,1,0:T(8,128)(2,1)S(1)}, bf16[2,8,3072]{2,1,0:T(8,128)(2,1)S(1)}, u32[]{:S(2)}, u32[]{:S(2)}) collective-permute-start(bf16[2,8,3072]{2,1,0:T(8,128)(2,1)S(1)} %pad_maximum_fusion.1), channel_id=1, source_target_pairs={{0,12},{1,13},{2,14},{3,15},{4,0},{5,1},{6,2},{7,3},{8,4},{9,5},{1... | collective-permute-start | bytes 294920 | tf_op jit(solution)/shard_map/ppermute | solution.py:498
  19.1 1.9 %slice-start.3 = ((bf16[8192,4,128]{2,1,0:T(4,128)(2,1)}), bf16[3072,4,128]{2,1,0:T(4,128)(2,1)S(1)}, s32[]{:S(2)}) async-start(bf16[8192,4,128]{2,1,0:T(4,128)(2,1)} %param.13), calls=%async_computation.3 | async-start | bytes 6291456 | tf_op jit(solution)/shard_map/slice | solution.py:528
  21.5 8.2 %collective-permute-start.4 = (bf16[32,5120]{1,0:T(8,128)(2,1)S(1)}, bf16[32,5120]{1,0:T(8,128)(2,1)S(1)}, u32[]{:S(2)}, u32[]{:S(2)}) collective-permute-start(bf16[32,5120]{1,0:T(8,128)(2,1)S(1)} %bitcast.72), channel_id=1, source_target_pairs={{0,2},{1,3},{2,0},{3,1},{4,6},{5,7},{6,4},{7,5},{8,10},{9,11},{10,... | collective-permute-start | bytes 983048 | tf_op jit(solution)/shard_map/ppermute | solution.py:498
  29.7 2.7 %collective-permute-start.10 = (bf16[64,3072]{1,0:T(8,128)(2,1)S(1)}, bf16[64,3072]{1,0:T(8,128)(2,1)S(1)}, u32[]{:S(2)}, u32[]{:S(2)}) collective-permute-start(bf16[64,3072]{1,0:T(8,128)(2,1)S(1)} %bitcast.69), channel_id=1, source_target_pairs={{0,1},{1,0},{2,3},{3,2},{4,5},{5,4},{6,7},{7,6},{8,9},{9,8},{10,11... | collective-permute-start | bytes 1179656 | tf_op jit(solution)/shard_map/ppermute | solution.py:498
  29.7 2.2 %collective-permute-start.8 = (bf16[32,5120]{1,0:T(8,128)(2,1)S(1)}, bf16[32,5120]{1,0:T(8,128)(2,1)S(1)}, u32[]{:S(2)}, u32[]{:S(2)}) collective-permute-start(bf16[32,5120]{1,0:T(8,128)(2,1)S(1)} %bitcast.73), channel_id=1, source_target_pairs={{0,1},{1,0},{2,3},{3,2},{4,5},{5,4},{6,7},{7,6},{8,9},{9,8},{10,11... | collective-permute-start | bytes 983048 | tf_op jit(solution)/shard_map/ppermute | solution.py:498
  30.2 2.1 %collective-permute-start.9 = (bf16[32,5120]{1,0:T(8,128)(2,1)S(1)}, bf16[32,5120]{1,0:T(8,128)(2,1)S(1)}, u32[]{:S(2)}, u32[]{:S(2)}) collective-permute-start(bf16[32,5120]{1,0:T(8,128)(2,1)S(1)} %collective-permute-done.4.a1), channel_id=1, source_target_pairs={{0,1},{1,0},{2,3},{3,2},{4,5},{5,4},{6,7},{7,6},{8,9},{9,8},{10,11... | collective-permute-start | bytes 983048 | tf_op jit(solution)/shard_map/ppermute | solution.py:498
  32.9 1.9 %collective-permute-start.11 = (bf16[128,1024]{1,0:T(8,128)(2,1)S(1)}, bf16[128,1024]{1,0:T(8,128)(2,1)S(1)}, u32[]{:S(2)}, u32[]{:S(2)}) collective-permute-start(bf16[128,1024]{1,0:T(8,128)(2,1)S(1)} %get-tuple-element.47), channel_id=1, source_target_pairs={{0,1},{1,0},{2,3},{3,2},{4,5},{5,4},{6,7},{7,6},{8,9},{9,8},{10,11... | collective-permute-start | bytes 786440 | tf_op jit(solution)/shard_map/ppermute | solution.py:498
  34.8 17.3 %copy-start = (bf16[1,6,2048,128]{3,2,1,0:T(8,128)(2,1)S(1)}, bf16[1,6,2048,128]{3,2,1,0:T(8,128)(2,1)}, u32[]{:S(2)}) copy-start(bf16[1,6,2048,128]{3,2,1,0:T(8,128)(2,1)} %refs_4_.1) | copy-start | bytes 9437188
  34.8 17.3 %copy-start.1 = (bf16[1,6,2048,128]{3,2,1,0:T(8,128)(2,1)S(1)}, bf16[1,6,2048,128]{3,2,1,0:T(8,128)(2,1)}, u32[]{:S(2)}) copy-start(bf16[1,6,2048,128]{3,2,1,0:T(8,128)(2,1)} %refs_5_.1) | copy-start | bytes 9437188
  34.8 17.3 %copy-start.5 = (s32[128]{0:T(128)S(1)}, s32[128]{0:T(128)}, u32[]{:S(2)}) copy-start(s32[128]{0:T(128)} %lens_ref.1) | copy-start | bytes 1540
  34.8 17.3 %copy-start.6 = (s32[12]{0:T(128)S(1)}, s32[12]{0:T(128)}, u32[]{:S(2)}) copy-start(s32[12]{0:T(128)} %counts_ref.1) | copy-start | bytes 148
  35.0 5.9 %collective-permute-start.12 = (bf16[128,512]{1,0:T(8,128)(2,1)S(1)}, bf16[128,512]{1,0:T(8,128)(2,1)S(1)}, u32[]{:S(2)}, u32[]{:S(2)}) collective-permute-start(bf16[128,512]{1,0:T(8,128)(2,1)S(1)} %pad_maximum_fusion), channel_id=1, source_target_pairs={{0,2},{1,3},{2,0},{3,1},{4,6},{5,7},{6,4},{7,5},{8,10},{9,11},{10,... | collective-permute-start | bytes 393224 | tf_op jit(solution)/shard_map/ppermute | solution.py:498
  40.9 5.7 %collective-permute-start.13 = (bf16[128,256]{1,0:T(8,128)(2,1)S(1)}, bf16[128,256]{1,0:T(8,128)(2,1)S(1)}, u32[]{:S(2)}, u32[]{:S(2)}) collective-permute-start(bf16[128,256]{1,0:T(8,128)(2,1)S(1)} %slice.133), channel_id=1, source_target_pairs={{0,4},{1,5},{2,6},{3,7},{4,0},{5,1},{6,2},{7,3},{8,12},{9,13},{10,... | collective-permute-start | bytes 196616 | tf_op jit(solution)/shard_map/ppermute | solution.py:498
  41.2 5.4 %collective-permute-start.14 = (bf16[128,512]{1,0:T(8,128)(2,1)S(1)}, bf16[128,512]{1,0:T(8,128)(2,1)S(1)}, u32[]{:S(2)}, u32[]{:S(2)}) collective-permute-start(bf16[128,512]{1,0:T(8,128)(2,1)S(1)} %shard_map.112), channel_id=1, source_target_pairs={{0,0},{1,8},{2,1},{3,9},{4,2},{5,10},{6,3},{7,11},{8,4},{9,12},{10... | collective-permute-start | bytes 393224 | tf_op jit(solution)/shard_map/ppermute | solution.py:498
  41.9 10.2 %collective-permute-start.16 = (bf16[128,512]{1,0:T(8,128)(2,1)S(1)}, bf16[128,512]{1,0:T(8,128)(2,1)S(1)}, u32[]{:S(2)}, u32[]{:S(2)}) collective-permute-start(bf16[128,512]{1,0:T(8,128)(2,1)S(1)} %shard_map.112), channel_id=1, source_target_pairs={{0,8},{1,0},{2,9},{3,1},{4,10},{5,2},{6,11},{7,3},{8,12},{9,4},{10... | collective-permute-start | bytes 393224 | tf_op jit(solution)/shard_map/ppermute | solution.py:498
  46.6 27.9 %slice-start = ((s8[8388608]{0:T(1024)(128)(4,1)}), s8[4194304]{0:T(1024)(128)(4,1)S(1)}, s32[]{:S(2)}) async-start(s8[8388608]{0:T(1024)(128)(4,1)} %bitcast.63), calls=%async_computation | async-start | bytes 8388608
  46.6 27.9 %slice-start.1 = ((s8[8388608]{0:T(1024)(128)(4,1)}), s8[4194304]{0:T(1024)(128)(4,1)S(1)}, s32[]{:S(2)}) async-start(s8[8388608]{0:T(1024)(128)(4,1)} %bitcast.63), calls=%async_computation.1 | async-start | bytes 8388608
  46.7 16.4 %collective-permute-start.15 = (bf16[128,256]{1,0:T(8,128)(2,1)S(1)}, bf16[128,256]{1,0:T(8,128)(2,1)S(1)}, u32[]{:S(2)}, u32[]{:S(2)}) collective-permute-start(bf16[128,256]{1,0:T(8,128)(2,1)S(1)} %convert_element_type.101), channel_id=1, source_target_pairs={{0,8},{1,9},{2,10},{3,11},{4,12},{5,13},{6,14},{7,15},{8,0},{9,1},... | collective-permute-start | bytes 196616 | tf_op jit(solution)/shard_map/ppermute | solution.py:498
  66.2 5.0 %collective-permute-start.17 = (bf16[128,512]{1,0:T(8,128)(2,1)S(1)}, bf16[128,512]{1,0:T(8,128)(2,1)S(1)}, u32[]{:S(2)}, u32[]{:S(2)}) collective-permute-start(bf16[128,512]{1,0:T(8,128)(2,1)S(1)} %get-tuple-element.61), channel_id=1, source_target_pairs={{0,0},{8,1},{1,2},{9,3},{2,4},{10,5},{3,6},{11,7},{4,8},{12,9},{5,... | collective-permute-start | bytes 393224 | tf_op jit(solution)/shard_map/ppermute | solution.py:498
  66.9 7.7 %collective-permute-start.18 = (bf16[128,512]{1,0:T(8,128)(2,1)S(1)}, bf16[128,512]{1,0:T(8,128)(2,1)S(1)}, u32[]{:S(2)}, u32[]{:S(2)}) collective-permute-start(bf16[128,512]{1,0:T(8,128)(2,1)S(1)} %get-tuple-element.62), channel_id=1, source_target_pairs={{8,0},{0,1},{9,2},{1,3},{10,4},{2,5},{11,6},{3,7},{12,8},{4,9},{13... | collective-permute-start | bytes 393224 | tf_op jit(solution)/shard_map/ppermute | solution.py:498
  75.9 1.8 %collective-permute-start.24 = (bf16[64,3072]{1,0:T(8,128)(2,1)S(1)}, bf16[64,3072]{1,0:T(8,128)(2,1)S(1)}, u32[]{:S(2)}, u32[]{:S(2)}) collective-permute-start(bf16[64,3072]{1,0:T(8,128)(2,1)S(1)} %get-tuple-element.68), channel_id=1, source_target_pairs={{0,1},{1,0},{2,3},{3,2},{4,5},{5,4},{6,7},{7,6},{8,9},{9,8},{10,11... | collective-permute-start | bytes 1179656 | tf_op jit(solution)/shard_map/ppermute | solution.py:498
  77.8 10.0 %collective-permute-start.25 = (bf16[2,8,3072]{2,1,0:T(8,128)(2,1)S(1)}, bf16[2,8,3072]{2,1,0:T(8,128)(2,1)S(1)}, u32[]{:S(2)}, u32[]{:S(2)}) collective-permute-start(bf16[2,8,3072]{2,1,0:T(8,128)(2,1)S(1)} %get-tuple-element.73), channel_id=1, source_target_pairs={{0,4},{1,5},{2,6},{3,7},{4,8},{5,9},{6,10},{7,11},{8,12},{9,13},{1... | collective-permute-start | bytes 294920 | tf_op jit(solution)/shard_map/ppermute | solution.py:498
  82.7 9.0 %collective-permute-start.26 = (bf16[2,8,3072]{2,1,0:T(8,128)(2,1)S(1)}, bf16[2,8,3072]{2,1,0:T(8,128)(2,1)S(1)}, u32[]{:S(2)}, u32[]{:S(2)}) collective-permute-start(bf16[2,8,3072]{2,1,0:T(8,128)(2,1)S(1)} %get-tuple-element.74), channel_id=1, source_target_pairs={{0,8},{1,9},{2,10},{3,11},{4,12},{5,13},{6,14},{7,15},{8,0},{9,1},... | collective-permute-start | bytes 294920 | tf_op jit(solution)/shard_map/ppermute | solution.py:498
  84.7 27.2 %copy-start.3 = (bf16[8,8192]{1,0:T(8,128)(2,1)S(1)}, bf16[8,8192]{1,0:T(8,128)(2,1)}, u32[]{:S(2)}) copy-start(bf16[8,8192]{1,0:T(8,128)(2,1)} %x_ref.1) | copy-start | bytes 393220
  84.7 7.1 %collective-permute-start.27 = (bf16[2,8,3072]{2,1,0:T(8,128)(2,1)S(1)}, bf16[2,8,3072]{2,1,0:T(8,128)(2,1)S(1)}, u32[]{:S(2)}, u32[]{:S(2)}) collective-permute-start(bf16[2,8,3072]{2,1,0:T(8,128)(2,1)S(1)} %get-tuple-element.75), channel_id=1, source_target_pairs={{0,12},{1,13},{2,14},{3,15},{4,0},{5,1},{6,2},{7,3},{8,4},{9,5},{1... | collective-permute-start | bytes 294920 | tf_op jit(solution)/shard_map/ppermute | solution.py:498
  87.4 4.4 %collective-permute-start.19 = (bf16[64,5120]{1,0:T(8,128)(2,1)S(1)}, bf16[64,5120]{1,0:T(8,128)(2,1)S(1)}, u32[]{:S(2)}, u32[]{:S(2)}) collective-permute-start(bf16[64,5120]{1,0:T(8,128)(2,1)S(1)} %get-tuple-element.66), channel_id=1, source_target_pairs={{0,1},{1,0},{2,3},{3,2},{4,5},{5,4},{6,7},{7,6},{8,9},{9,8},{10,11... | collective-permute-start | bytes 1966088 | tf_op jit(solution)/shard_map/ppermute | solution.py:498
  91.9 10.2 %collective-permute-start.20 = (bf16[32,5120]{1,0:T(8,128)(2,1)S(1)}, bf16[32,5120]{1,0:T(8,128)(2,1)S(1)}, u32[]{:S(2)}, u32[]{:S(2)}) collective-permute-start(bf16[32,5120]{1,0:T(8,128)(2,1)S(1)} %add_convert_fusion.2), channel_id=1, source_target_pairs={{0,2},{1,3},{2,0},{3,1},{4,6},{5,7},{6,4},{7,5},{8,10},{9,11},{10,... | collective-permute-start | bytes 983048 | tf_op jit(solution)/shard_map/ppermute | solution.py:498
  92.9 14.4 %collective-permute-start.28 = (bf16[8,3072]{1,0:T(8,128)(2,1)S(1)}, bf16[8,3072]{1,0:T(8,128)(2,1)S(1)}, u32[]{:S(2)}, u32[]{:S(2)}) collective-permute-start(bf16[8,3072]{1,0:T(8,128)(2,1)S(1)} %fusion.4), channel_id=1, source_target_pairs={{0,2},{1,3},{2,0},{3,1},{4,6},{5,7},{6,4},{7,5},{8,10},{9,11},{10,... | collective-permute-start | bytes 147464 | tf_op jit(solution)/shard_map/ppermute | solution.py:498
  102.2 6.8 %collective-permute-start.21 = (bf16[8,5120]{1,0:T(8,128)(2,1)S(1)}, bf16[8,5120]{1,0:T(8,128)(2,1)S(1)}, u32[]{:S(2)}, u32[]{:S(2)}) collective-permute-start(bf16[8,5120]{1,0:T(8,128)(2,1)S(1)} %get-tuple-element.76), channel_id=1, source_target_pairs={{0,4},{1,5},{2,6},{3,7},{4,8},{5,9},{6,10},{7,11},{8,12},{9,13},{1... | collective-permute-start | bytes 245768 | tf_op jit(solution)/shard_map/ppermute | solution.py:498
  104.9 6.9 %collective-permute-start.22 = (bf16[8,5120]{1,0:T(8,128)(2,1)S(1)}, bf16[8,5120]{1,0:T(8,128)(2,1)S(1)}, u32[]{:S(2)}, u32[]{:S(2)}) collective-permute-start(bf16[8,5120]{1,0:T(8,128)(2,1)S(1)} %get-tuple-element.78), channel_id=1, source_target_pairs={{0,8},{1,9},{2,10},{3,11},{4,12},{5,13},{6,14},{7,15},{8,0},{9,1},... | collective-permute-start | bytes 245768 | tf_op jit(solution)/shard_map/ppermute | solution.py:498
  105.7 6.1 %collective-permute-start.23 = (bf16[8,5120]{1,0:T(8,128)(2,1)S(1)}, bf16[8,5120]{1,0:T(8,128)(2,1)S(1)}, u32[]{:S(2)}, u32[]{:S(2)}) collective-permute-start(bf16[8,5120]{1,0:T(8,128)(2,1)S(1)} %get-tuple-element.77), channel_id=1, source_target_pairs={{0,12},{1,13},{2,14},{3,15},{4,0},{5,1},{6,2},{7,3},{8,4},{9,5},{1... | collective-permute-start | bytes 245768 | tf_op jit(solution)/shard_map/ppermute | solution.py:498
